TPU v7x, 512 devices: a whole 4x4x16 slice. The times are simulated.
512 devices in a mesh: tx: 64 (over x, z), ty: 8 (over y, core).
Axes of the slice: x: 4, y: 4, z: 16, core: 2. Of those that a mesh axis runs over, the one named last changes fastest.
Arguments:
- forcing: float32 [3, 6, 1024, 1024], P(None, None, 'tx', 'ty'), may hold values from -6 to 6
- start_state: float32 [3, 6, 1024, 1024], P(None, None, 'tx', 'ty'), may hold values from -4 to 4
- ice_mask: int32 [1024, 1024], P('tx', 'ty'), may hold values from 0 to 2
- class_ids: int32 [6, 1024, 1024], P(None, 'tx', 'ty'), may hold values from 0 to 15
- eta_table: float32 [16], replicated, may hold values from 0.1 to 10
- friction: float32 [1024, 1024], P('tx', 'ty'), may hold values from 0.3 to 30
Outputs:
- adjoint: float32 [3, 6, 1024, 1024], P(None, None, 'tx', 'ty')
- residual: float32 [3, 6, 1024, 1024], P(None, None, 'tx', 'ty')
Inputs may be any that keep to these rules, and one draw needn't show every extreme that they name: `ice_mask`: 0 marks an ocean column, 1 a grounded one, 2 a floating one. `class_ids`: an index into eta_table.
All inputs are finite; a program needn't handle non-finite values.
Results may differ from a plain program's by a relative error of at most 0.00002.
Values sent between devices are 32-bit elements; how exact they have to be, the bound alone decides.
A program may use at most 64 MiB of HBM per device.

v0:
```python
import jax
import jax.numpy as jnp
from jax import lax
from jax.sharding import PartitionSpec as P

SWEEPS = 2
COARSE_SWEEPS = 4


DAMPING = 0.6
VERTICAL = 2.0
REACTION = 0.05


def extended(block, sides, width):
    for axis, dim in sides:
        count = lax.axis_size(axis)
        forward = [(i, i + 1) for i in range(count - 1)]
        backward = [(target, source) for source, target in forward]
        low = lax.ppermute(
            lax.slice_in_dim(block, block.shape[dim] - width, None, axis=dim), axis, forward
        )
        high = lax.ppermute(lax.slice_in_dim(block, 0, width, axis=dim), axis, backward)
        block = jnp.concatenate([low, block, high], axis=dim)
    return block


def stencil_terms():
    terms = []
    for step_z in (-1, 0, 1):
        for step_x in (-1, 0, 1):
            for step_y in (-1, 0, 1):
                nonzero_axes = abs(step_z) + abs(step_x) + abs(step_y)
                if nonzero_axes > 0:
                    terms.append((step_z, step_x, step_y, nonzero_axes))
    return terms


def apply_operator(padded, coef_pad, spacing, ocean_weight):
    layers = padded.shape[1]
    width_x = padded.shape[2] - 2
    width_y = padded.shape[3] - 2
    viscosity = coef_pad[:layers]
    active = jnp.broadcast_to(coef_pad[layers], viscosity.shape)
    basal = coef_pad[layers + 1]
    visc_z = jnp.pad(viscosity, ((1, 1), (0, 0), (0, 0)))
    active_z = jnp.pad(active, ((1, 1), (0, 0), (0, 0)))
    field_z = jnp.pad(padded, ((0, 0), (1, 1), (0, 0), (0, 0)))
    visc_mid = viscosity[:, 1 : 1 + width_x, 1 : 1 + width_y]
    active_mid = active[:, 1 : 1 + width_x, 1 : 1 + width_y]
    coupled = jnp.zeros((3, layers, width_x, width_y), jnp.float32)
    weight_sum = jnp.zeros((3, layers, width_x, width_y), jnp.float32)
    for step_z, step_x, step_y, nonzero_axes in stencil_terms():
        base_weight = (
            0.25 ** (nonzero_axes - 1)
            * VERTICAL ** abs(step_z)
            * spacing ** (abs(step_x) + abs(step_y))
        )
        factors = (
            jnp.array(
                [1.0 + abs(step_x), 1.0 + abs(step_y), 1.0 + abs(step_z)], jnp.float32
            ).reshape(3, 1, 1, 1)
            * base_weight
        )
        z_range = slice(1 + step_z, 1 + step_z + layers)
        x_range = slice(1 + step_x, 1 + step_x + width_x)
        y_range = slice(1 + step_y, 1 + step_y + width_y)
        pair_mean = (
            0.5
            * (visc_mid + visc_z[z_range, x_range, y_range])
            * active_mid
            * active_z[z_range, x_range, y_range]
        )
        links = factors * pair_mean[None]
        coupled = coupled + links * field_z[:, z_range, x_range, y_range]
        weight_sum = weight_sum + links
    layer_ids = lax.broadcasted_iota(jnp.int32, (3, layers, 1, 1), 1)
    comp_ids = lax.broadcasted_iota(jnp.int32, (3, layers, 1, 1), 0)
    bottom = jnp.where((layer_ids == 0) & (comp_ids < 2), 1.0, 0.0).astype(jnp.float32)
    basal_term = bottom * basal[None, None, 1 : 1 + width_x, 1 : 1 + width_y]
    diagonal = (
        weight_sum
        + (REACTION * visc_mid * active_mid + ocean_weight * (1.0 - active_mid))[None]
        + basal_term
    )
    centre = padded[:, :, 1 : 1 + width_x, 1 : 1 + width_y]
    return (diagonal * centre - coupled, diagonal)


def jacobi_sweep(padded, right_side, coef_pad, spacing, ocean_weight):
    applied, diagonal = apply_operator(padded, coef_pad, spacing, ocean_weight)
    centre = padded[:, :, 1:-1, 1:-1]
    return centre + DAMPING * (right_side - applied) / diagonal


def build_coefficients(class_ids, eta_table, ice_mask, friction):
    levels = lax.broadcasted_iota(jnp.int32, (eta_table.shape[0], 1, 1, 1), 0)
    viscosity = jnp.sum(
        jnp.where(class_ids[None] == levels, eta_table[:, None, None, None], 0.0), axis=0
    )
    active = jnp.where(ice_mask != 0, 1.0, 0.0).astype(jnp.float32)
    basal = jnp.where(ice_mask == 1, friction, 0.0)
    return jnp.concatenate([viscosity, active[None], basal[None]], axis=0)


def coarsen_sum(values):
    leading = values.shape[:-2]
    shaped = values.reshape(leading + (values.shape[-2] // 2, 2, values.shape[-1] // 2, 2))
    return jnp.sum(shaped, axis=(-3, -1))


def coarse_coefficients(coefficients):
    layers = coefficients.shape[0] - 2
    summed = coarsen_sum(coefficients)
    return jnp.concatenate(
        [summed[:layers], 0.25 * summed[layers : layers + 1], summed[layers + 1 :]], axis=0
    )


def refine(values):
    return jnp.repeat(jnp.repeat(values, 2, axis=-2), 2, axis=-1)


def shards(forcing, start_state, ice_mask, class_ids, eta_table, friction):
    coefficients = build_coefficients(class_ids, eta_table, ice_mask, friction)
    coef_pad = extended(coefficients, (("tx", 1), ("ty", 2)), 1)

    def with_rims(iterate):
        return extended(iterate, (("tx", 2), ("ty", 3)), 1)

    def smooth_residual(iterate):
        for sweep_index in range(SWEEPS):
            iterate = jacobi_sweep(with_rims(iterate), forcing, coef_pad, 1.0, 1.0)
        applied, unused_diag = apply_operator(with_rims(iterate), coef_pad, 1.0, 1.0)
        return (iterate, forcing - applied)

    iterate, fine_residual = smooth_residual(start_state)
    coarse_rhs = coarsen_sum(fine_residual)
    coarse_coef = coarse_coefficients(coefficients)
    coarse_pad = extended(coarse_coef, (("tx", 1), ("ty", 2)), 1)
    correction = jnp.zeros_like(coarse_rhs)
    for sweep_index in range(COARSE_SWEEPS):
        correction = jacobi_sweep(
            extended(correction, (("tx", 2), ("ty", 3)), 1), coarse_rhs, coarse_pad, 0.5, 4.0
        )
    iterate = iterate + refine(correction)
    iterate, final_residual = smooth_residual(iterate)
    return (iterate, final_residual)


def solution(mesh):
    return jax.shard_map(
        shards,
        mesh=mesh,
        in_specs=(
            P(None, None, "tx", "ty"),
            P(None, None, "tx", "ty"),
            P("tx", "ty"),
            P(None, "tx", "ty"),
            P(),
            P("tx", "ty"),
        ),
        out_specs=(P(None, None, "tx", "ty"), P(None, None, "tx", "ty")),
        check_vma=False,
    )
```

profile of v0, /device:TPU:22, one launch (start us, length us, event | category | flops | bytes accessed | tf_op | source)
XLA Modules:
  0.0 266.5 jit_solution(1786471628765746130)
XLA Ops:
  0.6 11.7 %collective-permute-start.21 = (f32[3,6,1,64]{3,2,1,0:T(1,128)S(1)}, f32[3,6,1,64]{3,2,1,0:T(1,128)S(1)}, u32[]{:S(2)}, u32[]{:S(2)}) collective-permute-start(f32[3,6,1,64]{3,2,1,0:T(1,128)S(1)} %broadcast.817), channel_id=1, source_target_pairs={{8,0},{16,8},{24,16},{32,24},{40,32},{48,40},{56,48},{64,56},{72,6... | collective-permute-start | bytes 13832 | tf_op jit(solution)/shard_map/ppermute | solution.py:23
  15.8 6.0 %collective-permute-start.5 = (f32[3,6,1,128]{3,2,1,0:T(1,128)}, f32[3,6,1,128]{3,2,1,0:T(1,128)}, u32[]{:S(2)}, u32[]{:S(2)}) collective-permute-start(f32[3,6,1,128]{3,2,1,0:T(1,128)} %get-tuple-element.93), channel_id=1, source_target_pairs={{8,0},{16,8},{24,16},{32,24},{40,32},{48,40},{56,48},{64,56},{72,6... | collective-permute-start | bytes 27656 | tf_op jit(solution)/shard_map/ppermute | solution.py:23
  27.0 2.2 maximum_reduce_fusion
  29.8 1.9 collective-permute-start.17
  31.8 3.9 %collective-permute-start.16 = (f32[8,1,64]{2,1,0:T(1,128)S(1)}, f32[8,1,64]{2,1,0:T(1,128)S(1)}, u32[]{:S(2)}, u32[]{:S(2)}) collective-permute-start(f32[8,1,64]{2,1,0:T(1,128)S(1)} %get-tuple-element.168), channel_id=1, source_target_pairs={{0,8},{8,16},{16,24},{24,32},{32,40},{40,48},{48,56},{56,64},{64,7... | collective-permute-start | bytes 6152 | tf_op jit(solution)/shard_map/ppermute | solution.py:20
  35.8 3.6 %collective-permute-done.16 = f32[8,1,64]{2,1,0:T(1,128)S(1)} collective-permute-done((f32[8,1,64]{2,1,0:T(1,128)S(1)}, f32[8,1,64]{2,1,0:T(1,128)S(1)}, u32[]{:S(2)}, u32[]{:S(2)}) %collective-permute-start.16) | collective-permute-done | bytes 2080 | tf_op jit(solution)/shard_map/ppermute | solution.py:20
  41.4 2.4 collective-permute-start.18
  46.7 3.0 %collective-permute-start = (f32[8,1,128]{2,1,0:T(1,128)S(1)}, f32[8,1,128]{2,1,0:T(1,128)S(1)}, u32[]{:S(2)}, u32[]{:S(2)}) collective-permute-start(f32[8,1,128]{2,1,0:T(1,128)S(1)} %get-tuple-element.151), channel_id=1, source_target_pairs={{0,8},{8,16},{16,24},{24,32},{32,40},{40,48},{48,56},{56,64},{64,7... | collective-permute-start | bytes 12296 | tf_op jit(solution)/shard_map/ppermute | solution.py:20
  55.9 2.6 collective-permute-start.3
  60.7 3.8 %collective-permute-done.2 = f32[8,18,1]{2,1,0:T(8,128)S(1)} collective-permute-done((f32[8,18,1]{2,1,0:T(8,128)S(1)}, f32[8,18,1]{2,1,0:T(8,128)S(1)}, u32[]{:S(2)}, u32[]{:S(2)}) %collective-permute-start.2) | collective-permute-done | bytes 608 | tf_op jit(solution)/shard_map/ppermute | solution.py:20
  66.9 1.9 collective-permute-start.7
  68.8 2.4 collective-permute-start.6
  72.2 3.8 %collective-permute-done.6 = f32[3,6,18,1]{3,2,1,0:T(8,128)S(1)} collective-permute-done((f32[3,6,18,1]{3,2,1,0:T(8,128)S(1)}, f32[3,6,18,1]{3,2,1,0:T(8,128)S(1)}, u32[]{:S(2)}, u32[]{:S(2)}) %collective-permute-start.6) | collective-permute-done | bytes 1328 | tf_op jit(solution)/shard_map/ppermute | solution.py:20
  80.0 5.8 %collective-permute-start.9 = (f32[3,6,1,128]{3,2,1,0:T(1,128)S(1)}, f32[3,6,1,128]{3,2,1,0:T(1,128)S(1)}, u32[]{:S(2)}, u32[]{:S(2)}) collective-permute-start(f32[3,6,1,128]{3,2,1,0:T(1,128)S(1)} %get-tuple-element.91), channel_id=1, source_target_pairs={{8,0},{16,8},{24,16},{32,24},{40,32},{48,40},{56,48},{64,56},{72,6... | collective-permute-start | bytes 27656 | tf_op jit(solution)/shard_map/ppermute | solution.py:23
  89.7 2.4 collective-permute-start.22
  95.5 2.4 collective-permute-start.10
  98.9 3.8 %collective-permute-done.10 = f32[3,6,18,1]{3,2,1,0:T(8,128)S(1)} collective-permute-done((f32[3,6,18,1]{3,2,1,0:T(8,128)S(1)}, f32[3,6,18,1]{3,2,1,0:T(8,128)S(1)}, u32[]{:S(2)}, u32[]{:S(2)}) %collective-permute-start.10) | collective-permute-done | bytes 1328 | tf_op jit(solution)/shard_map/ppermute | solution.py:20
  104.4 6.0 %collective-permute-start.13 = (f32[3,6,1,128]{3,2,1,0:T(1,128)S(1)}, f32[3,6,1,128]{3,2,1,0:T(1,128)S(1)}, u32[]{:S(2)}, u32[]{:S(2)}) collective-permute-start(f32[3,6,1,128]{3,2,1,0:T(1,128)S(1)} %get-tuple-element.89), channel_id=1, source_target_pairs={{8,0},{16,8},{24,16},{32,24},{40,32},{48,40},{56,48},{64,56},{72,6... | collective-permute-start | bytes 27656 | tf_op jit(solution)/shard_map/ppermute | solution.py:23
  110.4 2.1 collective-permute-start.12
  113.4 4.7 %collective-permute-done.12 = f32[3,6,1,128]{3,2,1,0:T(1,128)S(1)} collective-permute-done((f32[3,6,1,128]{3,2,1,0:T(1,128)S(1)}, f32[3,6,1,128]{3,2,1,0:T(1,128)S(1)}, u32[]{:S(2)}, u32[]{:S(2)}) %collective-permute-start.12) | collective-permute-done | bytes 9248 | tf_op jit(solution)/shard_map/ppermute | solution.py:20
  118.2 1.9 collective-permute-start.15
  120.1 2.4 collective-permute-start.14
  123.6 3.8 %collective-permute-done.14 = f32[3,6,18,1]{3,2,1,0:T(8,128)S(1)} collective-permute-done((f32[3,6,18,1]{3,2,1,0:T(8,128)S(1)}, f32[3,6,18,1]{3,2,1,0:T(8,128)S(1)}, u32[]{:S(2)}, u32[]{:S(2)}) %collective-permute-start.14) | collective-permute-done | bytes 1328 | tf_op jit(solution)/shard_map/ppermute | solution.py:20
  131.9 3.9 %reduce_sum.28 = f32[3,6,8,64]{1,3,2,0:T(8,128)} reduce(f32[3,6,8,2,64,2]{1,5,4,3,2,0:T(2,128)S(1)} %bitcast.21, f32[]{:T(128)} %constant.22.clone.1), dimensions={3,5}, to_apply=%region_1.2 | reduce | flops 27648 | bytes 184324 | tf_op jit(solution)/shard_map/reduce_sum | solution.py:109
  137.5 3.1 %fusion.313 = f32[3,6,8,64]{3,2,1,0:T(8,128)S(1)} fusion(f32[3,6,8,64]{3,2,1,0:T(8,128)S(1)} %copy.1227, f32[3,6,10,66]{3,2,1,0:T(8,128)} %copy.1220, f32[3,6,8,64]{3,1,2,0:T(8,128)} %get-tuple-element.204, f32[3,6,1,64]{3,2,1,0:T(1,128)} %copy-done.86, f32[3,6,8,64]{3,1,2,0:T(8,128)} %get-tuple-element.131, f32[3,6,8,64]{3,1,2,0:T(8,128)} %get-tuple-element.205, ...), kind=kLoop, calls=%fused_computation.824 | loop fusion | flops 940032 | bytes 685616 | tf_op jit(solution)/shard_map/div | solution.py:93
  142.6 6.0 %collective-permute-start.25 = (f32[3,6,1,64]{3,2,1,0:T(1,128)S(1)}, f32[3,6,1,64]{3,2,1,0:T(1,128)S(1)}, u32[]{:S(2)}, u32[]{:S(2)}) collective-permute-start(f32[3,6,1,64]{3,2,1,0:T(1,128)S(1)} %get-tuple-element.147), channel_id=1, source_target_pairs={{8,0},{16,8},{24,16},{32,24},{40,32},{48,40},{56,48},{64,56},{72,6... | collective-permute-start | bytes 13832 | tf_op jit(solution)/shard_map/ppermute | solution.py:23
  152.0 2.4 collective-permute-start.26
  154.4 3.8 %collective-permute-done.26 = f32[3,6,10,1]{3,1,2,0:T(8,128)S(1)} collective-permute-done((f32[3,6,10,1]{3,1,2,0:T(8,128)S(1)}, f32[3,6,10,1]{3,1,2,0:T(8,128)S(1)}, u32[]{:S(2)}, u32[]{:S(2)}) %collective-permute-start.26) | collective-permute-done | bytes 752 | tf_op jit(solution)/shard_map/ppermute | solution.py:20
  161.5 6.3 %collective-permute-start.29 = (f32[3,6,1,64]{3,2,1,0:T(1,128)S(1)}, f32[3,6,1,64]{3,2,1,0:T(1,128)S(1)}, u32[]{:S(2)}, u32[]{:S(2)}) collective-permute-start(f32[3,6,1,64]{3,2,1,0:T(1,128)S(1)} %get-tuple-element.145), channel_id=1, source_target_pairs={{8,0},{16,8},{24,16},{32,24},{40,32},{48,40},{56,48},{64,56},{72,6... | collective-permute-start | bytes 13832 | tf_op jit(solution)/shard_map/ppermute | solution.py:23
  171.1 2.4 collective-permute-start.30
  173.6 3.8 %collective-permute-done.30 = f32[3,6,10,1]{3,1,2,0:T(8,128)S(1)} collective-permute-done((f32[3,6,10,1]{3,1,2,0:T(8,128)S(1)}, f32[3,6,10,1]{3,1,2,0:T(8,128)S(1)}, u32[]{:S(2)}, u32[]{:S(2)}) %collective-permute-start.30) | collective-permute-done | bytes 752 | tf_op jit(solution)/shard_map/ppermute | solution.py:20
  180.3 6.3 %collective-permute-start.33 = (f32[3,6,1,64]{3,2,1,0:T(1,128)S(1)}, f32[3,6,1,64]{3,2,1,0:T(1,128)S(1)}, u32[]{:S(2)}, u32[]{:S(2)}) collective-permute-start(f32[3,6,1,64]{3,2,1,0:T(1,128)S(1)} %get-tuple-element.143), channel_id=1, source_target_pairs={{8,0},{16,8},{24,16},{32,24},{40,32},{48,40},{56,48},{64,56},{72,6... | collective-permute-start | bytes 13832 | tf_op jit(solution)/shard_map/ppermute | solution.py:23
  188.0 1.9 collective-permute-start.35
  190.0 2.4 collective-permute-start.34
  192.4 3.8 %collective-permute-done.34 = f32[3,6,10,1]{3,1,2,0:T(8,128)S(1)} collective-permute-done((f32[3,6,10,1]{3,1,2,0:T(8,128)S(1)}, f32[3,6,10,1]{3,1,2,0:T(8,128)S(1)}, u32[]{:S(2)}, u32[]{:S(2)}) %collective-permute-start.34) | collective-permute-done | bytes 752 | tf_op jit(solution)/shard_map/ppermute | solution.py:20
  198.5 6.3 %collective-permute-start.37 = (f32[3,6,1,128]{3,2,1,0:T(1,128)S(1)}, f32[3,6,1,128]{3,2,1,0:T(1,128)S(1)}, u32[]{:S(2)}, u32[]{:S(2)}) collective-permute-start(f32[3,6,1,128]{3,2,1,0:T(1,128)S(1)} %get-tuple-element.87), channel_id=1, source_target_pairs={{8,0},{16,8},{24,16},{32,24},{40,32},{48,40},{56,48},{64,56},{72,6... | collective-permute-start | bytes 27656 | tf_op jit(solution)/shard_map/ppermute | solution.py:23
  204.8 2.1 collective-permute-start.36
  207.0 5.5 %collective-permute-done.36 = f32[3,6,1,128]{3,2,1,0:T(1,128)S(1)} collective-permute-done((f32[3,6,1,128]{3,2,1,0:T(1,128)S(1)}, f32[3,6,1,128]{3,2,1,0:T(1,128)S(1)}, u32[]{:S(2)}, u32[]{:S(2)}) %collective-permute-start.36) | collective-permute-done | bytes 9248 | tf_op jit(solution)/shard_map/ppermute | solution.py:20
  214.6 2.4 collective-permute-start.38
  218.0 3.8 %collective-permute-done.38 = f32[3,6,18,1]{3,2,1,0:T(8,128)S(1)} collective-permute-done((f32[3,6,18,1]{3,2,1,0:T(8,128)S(1)}, f32[3,6,18,1]{3,2,1,0:T(8,128)S(1)}, u32[]{:S(2)}, u32[]{:S(2)}) %collective-permute-start.38) | collective-permute-done | bytes 1328 | tf_op jit(solution)/shard_map/ppermute | solution.py:20
  226.5 3.9 %collective-permute-start.40 = (f32[3,6,1,128]{3,2,1,0:T(1,128)S(1)}, f32[3,6,1,128]{3,2,1,0:T(1,128)S(1)}, u32[]{:S(2)}, u32[]{:S(2)}) collective-permute-start(f32[3,6,1,128]{3,2,1,0:T(1,128)S(1)} %get-tuple-element.84), channel_id=1, source_target_pairs={{0,8},{8,16},{16,24},{24,32},{32,40},{40,48},{48,56},{56,64},{64,7... | collective-permute-start | bytes 27656 | tf_op jit(solution)/shard_map/ppermute | solution.py:20
  230.4 3.7 %collective-permute-done.40 = f32[3,6,1,128]{3,2,1,0:T(1,128)S(1)} collective-permute-done((f32[3,6,1,128]{3,2,1,0:T(1,128)S(1)}, f32[3,6,1,128]{3,2,1,0:T(1,128)S(1)}, u32[]{:S(2)}, u32[]{:S(2)}) %collective-permute-start.40) | collective-permute-done | bytes 9248 | tf_op jit(solution)/shard_map/ppermute | solution.py:20
  236.3 2.4 collective-permute-start.42
  239.7 3.8 %collective-permute-done.42 = f32[3,6,18,1]{3,2,1,0:T(8,128)S(1)} collective-permute-done((f32[3,6,18,1]{3,2,1,0:T(8,128)S(1)}, f32[3,6,18,1]{3,2,1,0:T(8,128)S(1)}, u32[]{:S(2)}, u32[]{:S(2)}) %collective-permute-start.42) | collective-permute-done | bytes 1328 | tf_op jit(solution)/shard_map/ppermute | solution.py:20
  247.1 3.9 %collective-permute-start.44 = (f32[3,6,1,128]{3,2,1,0:T(1,128)S(1)}, f32[3,6,1,128]{3,2,1,0:T(1,128)S(1)}, u32[]{:S(2)}, u32[]{:S(2)}) collective-permute-start(f32[3,6,1,128]{3,2,1,0:T(1,128)S(1)} %get-tuple-element.82), channel_id=1, source_target_pairs={{0,8},{8,16},{16,24},{24,32},{32,40},{40,48},{48,56},{56,64},{64,7... | collective-permute-start | bytes 27656 | tf_op jit(solution)/shard_map/ppermute | solution.py:20
  251.1 3.7 %collective-permute-done.44 = f32[3,6,1,128]{3,2,1,0:T(1,128)S(1)} collective-permute-done((f32[3,6,1,128]{3,2,1,0:T(1,128)S(1)}, f32[3,6,1,128]{3,2,1,0:T(1,128)S(1)}, u32[]{:S(2)}, u32[]{:S(2)}) %collective-permute-start.44) | collective-permute-done | bytes 9248 | tf_op jit(solution)/shard_map/ppermute | solution.py:20
  256.9 2.4 collective-permute-start.46
  260.3 3.8 %collective-permute-done.46 = f32[3,6,18,1]{3,2,1,0:T(8,128)S(1)} collective-permute-done((f32[3,6,18,1]{3,2,1,0:T(8,128)S(1)}, f32[3,6,18,1]{3,2,1,0:T(8,128)S(1)}, u32[]{:S(2)}, u32[]{:S(2)}) %collective-permute-start.46) | collective-permute-done | bytes 1328 | tf_op jit(solution)/shard_map/ppermute | solution.py:20
  (384 shorter events, 84.5 us)
Async XLA Ops:
  0.6 57.8 %collective-permute-start.21 = (f32[3,6,1,64]{3,2,1,0:T(1,128)S(1)}, f32[3,6,1,64]{3,2,1,0:T(1,128)S(1)}, u32[]{:S(2)}, u32[]{:S(2)}) collective-permute-start(f32[3,6,1,64]{3,2,1,0:T(1,128)S(1)} %broadcast.817), channel_id=1, source_target_pairs={{8,0},{16,8},{24,16},{32,24},{40,32},{48,40},{56,48},{64,56},{72,6... | collective-permute-start | bytes 13832 | tf_op jit(solution)/shard_map/ppermute | solution.py:23
  12.3 48.1 %collective-permute-start.20 = (f32[3,6,1,64]{3,2,1,0:T(1,128)S(1)}, f32[3,6,1,64]{3,2,1,0:T(1,128)S(1)}, u32[]{:S(2)}, u32[]{:S(2)}) collective-permute-start(f32[3,6,1,64]{3,2,1,0:T(1,128)S(1)} %broadcast.817), channel_id=1, source_target_pairs={{0,8},{8,16},{16,24},{24,32},{32,40},{40,48},{48,56},{56,64},{64,7... | collective-permute-start | bytes 13832 | tf_op jit(solution)/shard_map/ppermute | solution.py:20
  15.8 50.2 %collective-permute-start.5 = (f32[3,6,1,128]{3,2,1,0:T(1,128)}, f32[3,6,1,128]{3,2,1,0:T(1,128)}, u32[]{:S(2)}, u32[]{:S(2)}) collective-permute-start(f32[3,6,1,128]{3,2,1,0:T(1,128)} %get-tuple-element.93), channel_id=1, source_target_pairs={{8,0},{16,8},{24,16},{32,24},{40,32},{48,40},{56,48},{64,56},{72,6... | collective-permute-start | bytes 27656 | tf_op jit(solution)/shard_map/ppermute | solution.py:23
  29.8 6.0 %collective-permute-start.17 = (f32[8,1,64]{2,1,0:T(1,128)S(1)}, f32[8,1,64]{2,1,0:T(1,128)S(1)}, u32[]{:S(2)}, u32[]{:S(2)}) collective-permute-start(f32[8,1,64]{2,1,0:T(1,128)S(1)} %get-tuple-element.169), channel_id=1, source_target_pairs={{8,0},{16,8},{24,16},{32,24},{40,32},{48,40},{56,48},{64,56},{72,6... | collective-permute-start | bytes 6152 | tf_op jit(solution)/shard_map/ppermute | solution.py:23
  31.8 7.6 %collective-permute-start.16 = (f32[8,1,64]{2,1,0:T(1,128)S(1)}, f32[8,1,64]{2,1,0:T(1,128)S(1)}, u32[]{:S(2)}, u32[]{:S(2)}) collective-permute-start(f32[8,1,64]{2,1,0:T(1,128)S(1)} %get-tuple-element.168), channel_id=1, source_target_pairs={{0,8},{8,16},{16,24},{24,32},{32,40},{40,48},{48,56},{56,64},{64,7... | collective-permute-start | bytes 6152 | tf_op jit(solution)/shard_map/ppermute | solution.py:20
  39.5 4.4 %collective-permute-start.19 = (f32[8,10,1]{2,0,1:T(8,128)S(1)}, f32[8,10,1]{2,0,1:T(8,128)S(1)}, u32[]{:S(2)}, u32[]{:S(2)}) collective-permute-start(f32[8,10,1]{2,0,1:T(8,128)S(1)} %get-tuple-element.165), channel_id=1, source_target_pairs={{1,0},{2,1},{3,2},{4,3},{5,4},{6,5},{7,6},{9,8},{10,9},{11,10},{12... | collective-permute-start | bytes 968 | tf_op jit(solution)/shard_map/ppermute | solution.py:23
  41.4 5.3 %collective-permute-start.18 = (f32[8,10,1]{2,0,1:T(8,128)S(1)}, f32[8,10,1]{2,0,1:T(8,128)S(1)}, u32[]{:S(2)}, u32[]{:S(2)}) collective-permute-start(f32[8,10,1]{2,0,1:T(8,128)S(1)} %get-tuple-element.164), channel_id=1, source_target_pairs={{0,1},{1,2},{2,3},{3,4},{4,5},{5,6},{6,7},{8,9},{9,10},{10,11},{11... | collective-permute-start | bytes 968 | tf_op jit(solution)/shard_map/ppermute | solution.py:20
  43.8 10.0 %collective-permute-start.1 = (f32[8,1,128]{2,1,0:T(1,128)S(1)}, f32[8,1,128]{2,1,0:T(1,128)S(1)}, u32[]{:S(2)}, u32[]{:S(2)}) collective-permute-start(f32[8,1,128]{2,1,0:T(1,128)S(1)} %get-tuple-element.152), channel_id=1, source_target_pairs={{8,0},{16,8},{24,16},{32,24},{40,32},{48,40},{56,48},{64,56},{72,6... | collective-permute-start | bytes 12296 | tf_op jit(solution)/shard_map/ppermute | solution.py:23
  46.7 9.0 %collective-permute-start = (f32[8,1,128]{2,1,0:T(1,128)S(1)}, f32[8,1,128]{2,1,0:T(1,128)S(1)}, u32[]{:S(2)}, u32[]{:S(2)}) collective-permute-start(f32[8,1,128]{2,1,0:T(1,128)S(1)} %get-tuple-element.151), channel_id=1, source_target_pairs={{0,8},{8,16},{16,24},{24,32},{32,40},{40,48},{48,56},{56,64},{64,7... | collective-permute-start | bytes 12296 | tf_op jit(solution)/shard_map/ppermute | solution.py:20
  53.8 12.1 %collective-permute-start.4 = (f32[3,6,1,128]{3,2,1,0:T(1,128)}, f32[3,6,1,128]{3,2,1,0:T(1,128)S(1)}, u32[]{:S(2)}, u32[]{:S(2)}) collective-permute-start(f32[3,6,1,128]{3,2,1,0:T(1,128)} %get-tuple-element.92), channel_id=1, source_target_pairs={{0,8},{8,16},{16,24},{24,32},{32,40},{40,48},{48,56},{56,64},{64,7... | collective-permute-start | bytes 27656 | tf_op jit(solution)/shard_map/ppermute | solution.py:20
  55.9 4.8 %collective-permute-start.3 = (f32[8,18,1]{2,1,0:T(8,128)S(1)}, f32[8,18,1]{2,1,0:T(8,128)S(1)}, u32[]{:S(2)}, u32[]{:S(2)}) collective-permute-start(f32[8,18,1]{2,1,0:T(8,128)S(1)} %get-tuple-element.140), channel_id=1, source_target_pairs={{1,0},{2,1},{3,2},{4,3},{5,4},{6,5},{7,6},{9,8},{10,9},{11,10},{12... | collective-permute-start | bytes 1736 | tf_op jit(solution)/shard_map/ppermute | solution.py:23
  58.5 5.9 %collective-permute-start.2 = (f32[8,18,1]{2,1,0:T(8,128)S(1)}, f32[8,18,1]{2,1,0:T(8,128)S(1)}, u32[]{:S(2)}, u32[]{:S(2)}) collective-permute-start(f32[8,18,1]{2,1,0:T(8,128)S(1)} %get-tuple-element.139), channel_id=1, source_target_pairs={{0,1},{1,2},{2,3},{3,4},{4,5},{5,6},{6,7},{8,9},{9,10},{10,11},{11... | collective-permute-start | bytes 1736 | tf_op jit(solution)/shard_map/ppermute | solution.py:20
  66.9 5.4 %collective-permute-start.7 = (f32[3,6,18,1]{3,2,1,0:T(8,128)S(1)}, f32[3,6,18,1]{3,2,1,0:T(8,128)S(1)}, u32[]{:S(2)}, u32[]{:S(2)}) collective-permute-start(f32[3,6,18,1]{3,2,1,0:T(8,128)S(1)} %get-tuple-element.65), channel_id=1, source_target_pairs={{1,0},{2,1},{3,2},{4,3},{5,4},{6,5},{7,6},{9,8},{10,9},{11,10},{12... | collective-permute-start | bytes 3896 | tf_op jit(solution)/shard_map/ppermute | solution.py:23
  68.8 7.3 %collective-permute-start.6 = (f32[3,6,18,1]{3,2,1,0:T(8,128)S(1)}, f32[3,6,18,1]{3,2,1,0:T(8,128)S(1)}, u32[]{:S(2)}, u32[]{:S(2)}) collective-permute-start(f32[3,6,18,1]{3,2,1,0:T(8,128)S(1)} %get-tuple-element.64), channel_id=1, source_target_pairs={{0,1},{1,2},{2,3},{3,4},{4,5},{5,6},{6,7},{8,9},{9,10},{10,11},{11... | collective-permute-start | bytes 3896 | tf_op jit(solution)/shard_map/ppermute | solution.py:20
  80.0 12.1 %collective-permute-start.9 = (f32[3,6,1,128]{3,2,1,0:T(1,128)S(1)}, f32[3,6,1,128]{3,2,1,0:T(1,128)S(1)}, u32[]{:S(2)}, u32[]{:S(2)}) collective-permute-start(f32[3,6,1,128]{3,2,1,0:T(1,128)S(1)} %get-tuple-element.91), channel_id=1, source_target_pairs={{8,0},{16,8},{24,16},{32,24},{40,32},{48,40},{56,48},{64,56},{72,6... | collective-permute-start | bytes 27656 | tf_op jit(solution)/shard_map/ppermute | solution.py:23
  85.7 7.7 %collective-permute-start.8 = (f32[3,6,1,128]{3,2,1,0:T(1,128)S(1)}, f32[3,6,1,128]{3,2,1,0:T(1,128)S(1)}, u32[]{:S(2)}, u32[]{:S(2)}) collective-permute-start(f32[3,6,1,128]{3,2,1,0:T(1,128)S(1)} %get-tuple-element.90), channel_id=1, source_target_pairs={{0,8},{8,16},{16,24},{24,32},{32,40},{40,48},{48,56},{56,64},{64,7... | collective-permute-start | bytes 27656 | tf_op jit(solution)/shard_map/ppermute | solution.py:20
  87.8 10.1 %collective-permute-start.23 = (f32[3,6,10,1]{3,1,2,0:T(8,128)S(1)}, f32[3,6,10,1]{3,1,2,0:T(8,128)S(1)}, u32[]{:S(2)}, u32[]{:S(2)}) collective-permute-start(f32[3,6,10,1]{3,1,2,0:T(8,128)S(1)} %get-tuple-element.138), channel_id=1, source_target_pairs={{1,0},{2,1},{3,2},{4,3},{5,4},{6,5},{7,6},{9,8},{10,9},{11,10},{12... | collective-permute-start | bytes 2168 | tf_op jit(solution)/shard_map/ppermute | solution.py:23
  89.7 8.2 %collective-permute-start.22 = (f32[3,6,10,1]{3,1,2,0:T(8,128)S(1)}, f32[3,6,10,1]{3,1,2,0:T(8,128)S(1)}, u32[]{:S(2)}, u32[]{:S(2)}) collective-permute-start(f32[3,6,10,1]{3,1,2,0:T(8,128)S(1)} %get-tuple-element.137), channel_id=1, source_target_pairs={{0,1},{1,2},{2,3},{3,4},{4,5},{5,6},{6,7},{8,9},{9,10},{10,11},{11... | collective-permute-start | bytes 2168 | tf_op jit(solution)/shard_map/ppermute | solution.py:20
  93.6 5.4 %collective-permute-start.11 = (f32[3,6,18,1]{3,2,1,0:T(8,128)S(1)}, f32[3,6,18,1]{3,2,1,0:T(8,128)S(1)}, u32[]{:S(2)}, u32[]{:S(2)}) collective-permute-start(f32[3,6,18,1]{3,2,1,0:T(8,128)S(1)} %get-tuple-element.63), channel_id=1, source_target_pairs={{1,0},{2,1},{3,2},{4,3},{5,4},{6,5},{7,6},{9,8},{10,9},{11,10},{12... | collective-permute-start | bytes 3896 | tf_op jit(solution)/shard_map/ppermute | solution.py:23
  95.5 7.3 %collective-permute-start.10 = (f32[3,6,18,1]{3,2,1,0:T(8,128)S(1)}, f32[3,6,18,1]{3,2,1,0:T(8,128)S(1)}, u32[]{:S(2)}, u32[]{:S(2)}) collective-permute-start(f32[3,6,18,1]{3,2,1,0:T(8,128)S(1)} %get-tuple-element.62), channel_id=1, source_target_pairs={{0,1},{1,2},{2,3},{3,4},{4,5},{5,6},{6,7},{8,9},{9,10},{10,11},{11... | collective-permute-start | bytes 3896 | tf_op jit(solution)/shard_map/ppermute | solution.py:20
  104.4 9.0 %collective-permute-start.13 = (f32[3,6,1,128]{3,2,1,0:T(1,128)S(1)}, f32[3,6,1,128]{3,2,1,0:T(1,128)S(1)}, u32[]{:S(2)}, u32[]{:S(2)}) collective-permute-start(f32[3,6,1,128]{3,2,1,0:T(1,128)S(1)} %get-tuple-element.89), channel_id=1, source_target_pairs={{8,0},{16,8},{24,16},{32,24},{40,32},{48,40},{56,48},{64,56},{72,6... | collective-permute-start | bytes 27656 | tf_op jit(solution)/shard_map/ppermute | solution.py:23
  110.4 7.7 %collective-permute-start.12 = (f32[3,6,1,128]{3,2,1,0:T(1,128)S(1)}, f32[3,6,1,128]{3,2,1,0:T(1,128)S(1)}, u32[]{:S(2)}, u32[]{:S(2)}) collective-permute-start(f32[3,6,1,128]{3,2,1,0:T(1,128)S(1)} %get-tuple-element.88), channel_id=1, source_target_pairs={{0,8},{8,16},{16,24},{24,32},{32,40},{40,48},{48,56},{56,64},{64,7... | collective-permute-start | bytes 27656 | tf_op jit(solution)/shard_map/ppermute | solution.py:20
  118.2 5.4 %collective-permute-start.15 = (f32[3,6,18,1]{3,2,1,0:T(8,128)S(1)}, f32[3,6,18,1]{3,2,1,0:T(8,128)S(1)}, u32[]{:S(2)}, u32[]{:S(2)}) collective-permute-start(f32[3,6,18,1]{3,2,1,0:T(8,128)S(1)} %get-tuple-element.61), channel_id=1, source_target_pairs={{1,0},{2,1},{3,2},{4,3},{5,4},{6,5},{7,6},{9,8},{10,9},{11,10},{12... | collective-permute-start | bytes 3896 | tf_op jit(solution)/shard_map/ppermute | solution.py:23
  120.1 7.3 %collective-permute-start.14 = (f32[3,6,18,1]{3,2,1,0:T(8,128)S(1)}, f32[3,6,18,1]{3,2,1,0:T(8,128)S(1)}, u32[]{:S(2)}, u32[]{:S(2)}) collective-permute-start(f32[3,6,18,1]{3,2,1,0:T(8,128)S(1)} %get-tuple-element.60), channel_id=1, source_target_pairs={{0,1},{1,2},{2,3},{3,4},{4,5},{5,6},{6,7},{8,9},{9,10},{10,11},{11... | collective-permute-start | bytes 3896 | tf_op jit(solution)/shard_map/ppermute | solution.py:20
  140.6 8.0 %collective-permute-start.24 = (f32[3,6,1,64]{3,2,1,0:T(1,128)S(1)}, f32[3,6,1,64]{3,2,1,0:T(1,128)S(1)}, u32[]{:S(2)}, u32[]{:S(2)}) collective-permute-start(f32[3,6,1,64]{3,2,1,0:T(1,128)S(1)} %get-tuple-element.148), channel_id=1, source_target_pairs={{0,8},{8,16},{16,24},{24,32},{32,40},{40,48},{48,56},{56,64},{64,7... | collective-permute-start | bytes 13832 | tf_op jit(solution)/shard_map/ppermute | solution.py:20
  142.6 7.4 %collective-permute-start.25 = (f32[3,6,1,64]{3,2,1,0:T(1,128)S(1)}, f32[3,6,1,64]{3,2,1,0:T(1,128)S(1)}, u32[]{:S(2)}, u32[]{:S(2)}) collective-permute-start(f32[3,6,1,64]{3,2,1,0:T(1,128)S(1)} %get-tuple-element.147), channel_id=1, source_target_pairs={{8,0},{16,8},{24,16},{32,24},{40,32},{48,40},{56,48},{64,56},{72,6... | collective-permute-start | bytes 13832 | tf_op jit(solution)/shard_map/ppermute | solution.py:23
  150.1 4.4 %collective-permute-start.27 = (f32[3,6,10,1]{3,1,2,0:T(8,128)S(1)}, f32[3,6,10,1]{3,1,2,0:T(8,128)S(1)}, u32[]{:S(2)}, u32[]{:S(2)}) collective-permute-start(f32[3,6,10,1]{3,1,2,0:T(8,128)S(1)} %get-tuple-element.126), channel_id=1, source_target_pairs={{1,0},{2,1},{3,2},{4,3},{5,4},{6,5},{7,6},{9,8},{10,9},{11,10},{12... | collective-permute-start | bytes 2168 | tf_op jit(solution)/shard_map/ppermute | solution.py:23
  152.0 6.2 %collective-permute-start.26 = (f32[3,6,10,1]{3,1,2,0:T(8,128)S(1)}, f32[3,6,10,1]{3,1,2,0:T(8,128)S(1)}, u32[]{:S(2)}, u32[]{:S(2)}) collective-permute-start(f32[3,6,10,1]{3,1,2,0:T(8,128)S(1)} %get-tuple-element.125), channel_id=1, source_target_pairs={{0,1},{1,2},{2,3},{3,4},{4,5},{5,6},{6,7},{8,9},{9,10},{10,11},{11... | collective-permute-start | bytes 2168 | tf_op jit(solution)/shard_map/ppermute | solution.py:20
  159.5 8.2 %collective-permute-start.28 = (f32[3,6,1,64]{3,2,1,0:T(1,128)S(1)}, f32[3,6,1,64]{3,2,1,0:T(1,128)S(1)}, u32[]{:S(2)}, u32[]{:S(2)}) collective-permute-start(f32[3,6,1,64]{3,2,1,0:T(1,128)S(1)} %get-tuple-element.146), channel_id=1, source_target_pairs={{0,8},{8,16},{16,24},{24,32},{32,40},{40,48},{48,56},{56,64},{64,7... | collective-permute-start | bytes 13832 | tf_op jit(solution)/shard_map/ppermute | solution.py:20
  161.5 7.7 %collective-permute-start.29 = (f32[3,6,1,64]{3,2,1,0:T(1,128)S(1)}, f32[3,6,1,64]{3,2,1,0:T(1,128)S(1)}, u32[]{:S(2)}, u32[]{:S(2)}) collective-permute-start(f32[3,6,1,64]{3,2,1,0:T(1,128)S(1)} %get-tuple-element.145), channel_id=1, source_target_pairs={{8,0},{16,8},{24,16},{32,24},{40,32},{48,40},{56,48},{64,56},{72,6... | collective-permute-start | bytes 13832 | tf_op jit(solution)/shard_map/ppermute | solution.py:23
  169.2 4.4 %collective-permute-start.31 = (f32[3,6,10,1]{3,1,2,0:T(8,128)S(1)}, f32[3,6,10,1]{3,1,2,0:T(8,128)S(1)}, u32[]{:S(2)}, u32[]{:S(2)}) collective-permute-start(f32[3,6,10,1]{3,1,2,0:T(8,128)S(1)} %get-tuple-element.121), channel_id=1, source_target_pairs={{1,0},{2,1},{3,2},{4,3},{5,4},{6,5},{7,6},{9,8},{10,9},{11,10},{12... | collective-permute-start | bytes 2168 | tf_op jit(solution)/shard_map/ppermute | solution.py:23
  171.1 6.2 %collective-permute-start.30 = (f32[3,6,10,1]{3,1,2,0:T(8,128)S(1)}, f32[3,6,10,1]{3,1,2,0:T(8,128)S(1)}, u32[]{:S(2)}, u32[]{:S(2)}) collective-permute-start(f32[3,6,10,1]{3,1,2,0:T(8,128)S(1)} %get-tuple-element.120), channel_id=1, source_target_pairs={{0,1},{1,2},{2,3},{3,4},{4,5},{5,6},{6,7},{8,9},{9,10},{10,11},{11... | collective-permute-start | bytes 2168 | tf_op jit(solution)/shard_map/ppermute | solution.py:20
  178.3 8.2 %collective-permute-start.32 = (f32[3,6,1,64]{3,2,1,0:T(1,128)S(1)}, f32[3,6,1,64]{3,2,1,0:T(1,128)S(1)}, u32[]{:S(2)}, u32[]{:S(2)}) collective-permute-start(f32[3,6,1,64]{3,2,1,0:T(1,128)S(1)} %get-tuple-element.144), channel_id=1, source_target_pairs={{0,8},{8,16},{16,24},{24,32},{32,40},{40,48},{48,56},{56,64},{64,7... | collective-permute-start | bytes 13832 | tf_op jit(solution)/shard_map/ppermute | solution.py:20
  180.3 7.7 %collective-permute-start.33 = (f32[3,6,1,64]{3,2,1,0:T(1,128)S(1)}, f32[3,6,1,64]{3,2,1,0:T(1,128)S(1)}, u32[]{:S(2)}, u32[]{:S(2)}) collective-permute-start(f32[3,6,1,64]{3,2,1,0:T(1,128)S(1)} %get-tuple-element.143), channel_id=1, source_target_pairs={{8,0},{16,8},{24,16},{32,24},{40,32},{48,40},{56,48},{64,56},{72,6... | collective-permute-start | bytes 13832 | tf_op jit(solution)/shard_map/ppermute | solution.py:23
  188.0 4.4 %collective-permute-start.35 = (f32[3,6,10,1]{3,1,2,0:T(8,128)S(1)}, f32[3,6,10,1]{3,1,2,0:T(8,128)S(1)}, u32[]{:S(2)}, u32[]{:S(2)}) collective-permute-start(f32[3,6,10,1]{3,1,2,0:T(8,128)S(1)} %get-tuple-element.116), channel_id=1, source_target_pairs={{1,0},{2,1},{3,2},{4,3},{5,4},{6,5},{7,6},{9,8},{10,9},{11,10},{12... | collective-permute-start | bytes 2168 | tf_op jit(solution)/shard_map/ppermute | solution.py:23
  190.0 6.2 %collective-permute-start.34 = (f32[3,6,10,1]{3,1,2,0:T(8,128)S(1)}, f32[3,6,10,1]{3,1,2,0:T(8,128)S(1)}, u32[]{:S(2)}, u32[]{:S(2)}) collective-permute-start(f32[3,6,10,1]{3,1,2,0:T(8,128)S(1)} %get-tuple-element.115), channel_id=1, source_target_pairs={{0,1},{1,2},{2,3},{3,4},{4,5},{5,6},{6,7},{8,9},{9,10},{10,11},{11... | collective-permute-start | bytes 2168 | tf_op jit(solution)/shard_map/ppermute | solution.py:20
  198.5 8.5 %collective-permute-start.37 = (f32[3,6,1,128]{3,2,1,0:T(1,128)S(1)}, f32[3,6,1,128]{3,2,1,0:T(1,128)S(1)}, u32[]{:S(2)}, u32[]{:S(2)}) collective-permute-start(f32[3,6,1,128]{3,2,1,0:T(1,128)S(1)} %get-tuple-element.87), channel_id=1, source_target_pairs={{8,0},{16,8},{24,16},{32,24},{40,32},{48,40},{56,48},{64,56},{72,6... | collective-permute-start | bytes 27656 | tf_op jit(solution)/shard_map/ppermute | solution.py:23
  204.8 7.7 %collective-permute-start.36 = (f32[3,6,1,128]{3,2,1,0:T(1,128)S(1)}, f32[3,6,1,128]{3,2,1,0:T(1,128)S(1)}, u32[]{:S(2)}, u32[]{:S(2)}) collective-permute-start(f32[3,6,1,128]{3,2,1,0:T(1,128)S(1)} %get-tuple-element.86), channel_id=1, source_target_pairs={{0,8},{8,16},{16,24},{24,32},{32,40},{40,48},{48,56},{56,64},{64,7... | collective-permute-start | bytes 27656 | tf_op jit(solution)/shard_map/ppermute | solution.py:20
  212.6 5.4 %collective-permute-start.39 = (f32[3,6,18,1]{3,2,1,0:T(8,128)S(1)}, f32[3,6,18,1]{3,2,1,0:T(8,128)S(1)}, u32[]{:S(2)}, u32[]{:S(2)}) collective-permute-start(f32[3,6,18,1]{3,2,1,0:T(8,128)S(1)} %get-tuple-element.59), channel_id=1, source_target_pairs={{1,0},{2,1},{3,2},{4,3},{5,4},{6,5},{7,6},{9,8},{10,9},{11,10},{12... | collective-permute-start | bytes 3896 | tf_op jit(solution)/shard_map/ppermute | solution.py:23
  214.6 7.3 %collective-permute-start.38 = (f32[3,6,18,1]{3,2,1,0:T(8,128)S(1)}, f32[3,6,18,1]{3,2,1,0:T(8,128)S(1)}, u32[]{:S(2)}, u32[]{:S(2)}) collective-permute-start(f32[3,6,18,1]{3,2,1,0:T(8,128)S(1)} %get-tuple-element.58), channel_id=1, source_target_pairs={{0,1},{1,2},{2,3},{3,4},{4,5},{5,6},{6,7},{8,9},{9,10},{10,11},{11... | collective-permute-start | bytes 3896 | tf_op jit(solution)/shard_map/ppermute | solution.py:20
  224.6 5.9 %collective-permute-start.41 = (f32[3,6,1,128]{3,2,1,0:T(1,128)S(1)}, f32[3,6,1,128]{3,2,1,0:T(1,128)S(1)}, u32[]{:S(2)}, u32[]{:S(2)}) collective-permute-start(f32[3,6,1,128]{3,2,1,0:T(1,128)S(1)} %get-tuple-element.85), channel_id=1, source_target_pairs={{8,0},{16,8},{24,16},{32,24},{40,32},{48,40},{56,48},{64,56},{72,6... | collective-permute-start | bytes 27656 | tf_op jit(solution)/shard_map/ppermute | solution.py:23
  226.5 7.7 %collective-permute-start.40 = (f32[3,6,1,128]{3,2,1,0:T(1,128)S(1)}, f32[3,6,1,128]{3,2,1,0:T(1,128)S(1)}, u32[]{:S(2)}, u32[]{:S(2)}) collective-permute-start(f32[3,6,1,128]{3,2,1,0:T(1,128)S(1)} %get-tuple-element.84), channel_id=1, source_target_pairs={{0,8},{8,16},{16,24},{24,32},{32,40},{40,48},{48,56},{56,64},{64,7... | collective-permute-start | bytes 27656 | tf_op jit(solution)/shard_map/ppermute | solution.py:20
  234.3 5.4 %collective-permute-start.43 = (f32[3,6,18,1]{3,2,1,0:T(8,128)S(1)}, f32[3,6,18,1]{3,2,1,0:T(8,128)S(1)}, u32[]{:S(2)}, u32[]{:S(2)}) collective-permute-start(f32[3,6,18,1]{3,2,1,0:T(8,128)S(1)} %get-tuple-element.57), channel_id=1, source_target_pairs={{1,0},{2,1},{3,2},{4,3},{5,4},{6,5},{7,6},{9,8},{10,9},{11,10},{12... | collective-permute-start | bytes 3896 | tf_op jit(solution)/shard_map/ppermute | solution.py:23
  236.3 7.3 %collective-permute-start.42 = (f32[3,6,18,1]{3,2,1,0:T(8,128)S(1)}, f32[3,6,18,1]{3,2,1,0:T(8,128)S(1)}, u32[]{:S(2)}, u32[]{:S(2)}) collective-permute-start(f32[3,6,18,1]{3,2,1,0:T(8,128)S(1)} %get-tuple-element.56), channel_id=1, source_target_pairs={{0,1},{1,2},{2,3},{3,4},{4,5},{5,6},{6,7},{8,9},{9,10},{10,11},{11... | collective-permute-start | bytes 3896 | tf_op jit(solution)/shard_map/ppermute | solution.py:20
  245.2 5.9 %collective-permute-start.45 = (f32[3,6,1,128]{3,2,1,0:T(1,128)S(1)}, f32[3,6,1,128]{3,2,1,0:T(1,128)S(1)}, u32[]{:S(2)}, u32[]{:S(2)}) collective-permute-start(f32[3,6,1,128]{3,2,1,0:T(1,128)S(1)} %get-tuple-element.83), channel_id=1, source_target_pairs={{8,0},{16,8},{24,16},{32,24},{40,32},{48,40},{56,48},{64,56},{72,6... | collective-permute-start | bytes 27656 | tf_op jit(solution)/shard_map/ppermute | solution.py:23
  247.1 7.7 %collective-permute-start.44 = (f32[3,6,1,128]{3,2,1,0:T(1,128)S(1)}, f32[3,6,1,128]{3,2,1,0:T(1,128)S(1)}, u32[]{:S(2)}, u32[]{:S(2)}) collective-permute-start(f32[3,6,1,128]{3,2,1,0:T(1,128)S(1)} %get-tuple-element.82), channel_id=1, source_target_pairs={{0,8},{8,16},{16,24},{24,32},{32,40},{40,48},{48,56},{56,64},{64,7... | collective-permute-start | bytes 27656 | tf_op jit(solution)/shard_map/ppermute | solution.py:20
  255.0 5.4 %collective-permute-start.47 = (f32[3,6,18,1]{3,2,1,0:T(8,128)S(1)}, f32[3,6,18,1]{3,2,1,0:T(8,128)S(1)}, u32[]{:S(2)}, u32[]{:S(2)}) collective-permute-start(f32[3,6,18,1]{3,2,1,0:T(8,128)S(1)} %get-tuple-element.55), channel_id=1, source_target_pairs={{1,0},{2,1},{3,2},{4,3},{5,4},{6,5},{7,6},{9,8},{10,9},{11,10},{12... | collective-permute-start | bytes 3896 | tf_op jit(solution)/shard_map/ppermute | solution.py:23
  256.9 7.3 %collective-permute-start.46 = (f32[3,6,18,1]{3,2,1,0:T(8,128)S(1)}, f32[3,6,18,1]{3,2,1,0:T(8,128)S(1)}, u32[]{:S(2)}, u32[]{:S(2)}) collective-permute-start(f32[3,6,18,1]{3,2,1,0:T(8,128)S(1)} %get-tuple-element.54), channel_id=1, source_target_pairs={{0,1},{1,2},{2,3},{3,4},{4,5},{5,6},{6,7},{8,9},{9,10},{10,11},{11... | collective-permute-start | bytes 3896 | tf_op jit(solution)/shard_map/ppermute | solution.py:20
  (103 other events, 3288.4 us)
where the time goes:
time: 268 us; the launch traced here: 266 us
  starting transfers between devices  145 us (54%)
  waiting for transfers between devices  70.5 us (26%)
  other arithmetic  33.5 us (12%)
  local copies, waits for them, and re-layouts  14.3 us (5%)
  between operations  3.46 us (1%)
    ppermute x24, starting transfers between devices, extended(): lax.ppermute(lax.slice_in_dim(block, 0, width, axis=dim), axis, backward)  85.8 us
    ppermute x24, waiting for transfers between devices, extended(): lax.ppermute(lax.slice_in_dim(block, block.shape[dim] - width, None, axis...  61.5 us
    ppermute x24, starting transfers between devices, extended(): lax.ppermute(lax.slice_in_dim(block, block.shape[dim] - width, None, axis...  58.9 us
    ppermute x24, waiting for transfers between devices, extended(): lax.ppermute(lax.slice_in_dim(block, 0, width, axis=dim), axis, backward)  9.02 us
    concatenate x32, other arithmetic, extended(): block = jnp.concatenate([low, block, high], axis=dim)  7.84 us
    add x7, other arithmetic, jacobi_sweep(): return centre + DAMPING * (right_side - applied) / diagonal  7.04 us
    reduce_sum x2, other arithmetic, coarsen_sum(): return jnp.sum(shaped, axis=(-3, -1))  6.13 us
  transfers between devices with their start and end apart: 48, of which 27 were waited for; matrix products, arithmetic and copies ran while one was open for 7% of the time, Pallas kernels for 0%

commit v1 on v0

v1 whole, which is shorter than its diff:
```python
import functools

import jax
import jax.numpy as jnp
from jax import lax
from jax.experimental import pallas as pl
from jax.experimental.pallas import tpu as pltpu
from jax.sharding import PartitionSpec as P

DAMPING = 0.6
REACTION = 0.05
NZ = 6
LX = 16
FO = 4
CO = 12
KO = 6
FROWS = LX + 2 * FO
CROWS = LX + 2 * CO
KROWS = LX // 2 + 2 * KO
PACK_A_OWN, PACK_A = 32, 48
PACK_B_OWN, PACK_B = 24, 40


def lanes():
    return lax.broadcasted_iota(jnp.int32, (8, 128), 1)


def layers():
    return lax.broadcasted_iota(jnp.int32, (8, 128), 0)


def rows(low, high, step, body):
    def run(i, carry):
        for k in range(step):
            body(low + i * step + k)
        return carry

    lax.fori_loop(0, (high - low) // step, run, 0)


def along_y(main, halo, weight, shift):
    m1, h1 = pltpu.roll(main, shift, 1), pltpu.roll(halo, shift, 1)
    m2, h2 = pltpu.roll(main, 128 - shift, 1), pltpu.roll(halo, 128 - shift, 1)
    first, last = lanes() < shift, lanes() >= 128 - shift
    near_main = jnp.where(first, h1, m1) + jnp.where(last, h2, m2)
    near_halo = jnp.where(first, m1, h1) + jnp.where(last, m2, h2)
    return main + weight * near_main, halo + weight * near_halo


def along_z(tile, weight):
    return tile + weight * (pltpu.roll(tile, 1, 0) + pltpu.roll(tile, 7, 0))


def pack(items):
    packed = pltpu.roll(items[0], 16, 1)
    for j in range(1, len(items)):
        packed = jnp.where(lanes() >= 32 * j, pltpu.roll(items[j], 16 + 32 * j, 1), packed)
    return packed


def unpack(from_left, from_right, count):
    both = jnp.where(lanes() % 32 < 16, from_left, from_right)
    return [pltpu.roll(both, 112 - 32 * j, 1) for j in range(count)]


def kernel(
    ntx, nty,
    eta, forcing, start, mask, classes, friction, out_u, out_r,
    u, f, cf, a, av, d, inv, ub, g, ka, kav, kv, kd, kinv, kr, kc,
    pa, pal, par, pb, pbl, pbr, send, recv,
):
    tx, ty = lax.axis_index("tx"), lax.axis_index("ty")
    up, down = lax.rem(tx + 1, ntx), lax.rem(tx + ntx - 1, ntx)
    right, left = lax.rem(ty + 1, nty), lax.rem(ty + nty - 1, nty)
    barrier = pltpu.get_barrier_semaphore()
    for where in ({"tx": up}, {"tx": down}, {"ty": right}, {"ty": left}):
        pl.semaphore_signal(barrier, inc=1, device_id=where, device_id_type=pl.DeviceIdType.MESH)

    zero = jnp.zeros((LX, 128), jnp.float32)
    for c in range(3):
        for z in range(8):
            u[0, c, FO : FO + LX, z, :] = start[c, z] if z < NZ else zero
            f[0, c, FO : FO + LX, z, :] = forcing[c, z] if z < NZ else zero
    for z in range(NZ):
        ids = classes[z]
        visc = jnp.zeros((LX, 128), jnp.float32)
        for k in range(eta.shape[0]):
            visc = jnp.where(ids == k, eta[k], visc)
        cf[0, CO : CO + LX, z, :] = visc
    kind = mask[...]
    cf[0, CO : CO + LX, 6, :] = jnp.where(kind != 0, 1.0, 0.0).astype(jnp.float32)
    cf[0, CO : CO + LX, 7, :] = jnp.where(kind == 1, friction[...], 0.0)

    used = [0]

    def copy(src, dst, where):
        k = used[0]
        used[0] += 1
        made = pltpu.make_async_remote_copy(
            src_ref=src, dst_ref=dst, send_sem=send.at[k], recv_sem=recv.at[k],
            device_id=where, device_id_type=pl.DeviceIdType.MESH,
        )
        made.start()
        return made

    def to_both_rows(make, first, count, own):
        top = copy(make(first + own - count, count), make(first - count, count), {"tx": up})
        low = copy(make(first, count), make(first + own, count), {"tx": down})
        return [top, low]

    def to_both_lanes(packed, from_left, from_right, first, count):
        part = pl.ds(first, count)
        return [
            copy(packed.at[part], from_left.at[part], {"ty": right}),
            copy(packed.at[part], from_right.at[part], {"ty": left}),
        ]

    def tri(ref):
        return lambda first, count: ref.at[0, :, pl.ds(first, count)]

    pl.semaphore_wait(barrier, 4)
    x_a = to_both_rows(tri(u), FO, 4, LX)
    x_a += to_both_rows(tri(f), FO, 2, LX)
    x_a += to_both_rows(lambda first, count: cf.at[0, pl.ds(first, count)], CO, 12, LX)

    def pack_u(x, slot):
        pa[slot] = pack([u[0, 0, x + FO], u[0, 1, x + FO], u[0, 2, x + FO], cf[0, x + CO]])

    def pack_f(x, slot):
        pa[slot] = pack([f[0, c, x + FO] for c in range(3)])

    def pack_k(x, slot):
        pa[slot] = pack([cf[0, x + CO + j] for j in range(4)])

    def unpack_u(x, slot):
        got = unpack(pal[slot], par[slot], 4)
        for c in range(3):
            u[1, c, x + FO] = got[c]
        cf[1, x + CO] = got[3]

    def unpack_f(x, slot):
        got = unpack(pal[slot], par[slot], 3)
        for c in range(3):
            f[1, c, x + FO] = got[c]

    def unpack_k(x, slot):
        got = unpack(pal[slot], par[slot], 4)
        for j in range(4):
            cf[1, x + CO + j] = got[j]

    def own_a(do_u, do_f):
        def body(x):
            do_u(x, x)
            do_f(x, x + LX)

        rows(0, LX, 4, body)

    def halo_a(do_u, do_f, do_k):
        for j in range(4):
            do_u(j - 4, 32 + j)
            do_u(LX + j, 36 + j)
        for j in range(2):
            do_f(j - 2, 40 + j)
            do_f(LX + j, 42 + j)
            do_k(4 * j - 12, 44 + j)
            do_k(LX + 4 + 4 * j, 46 + j)

    own_a(pack_u, pack_f)
    y_own = to_both_lanes(pa, pal, par, 0, PACK_A_OWN)
    for made in x_a:
        made.wait_recv()
    halo_a(pack_u, pack_f, pack_k)
    y_halo = to_both_lanes(pa, pal, par, PACK_A_OWN, PACK_A - PACK_A_OWN)
    for made in y_own:
        made.wait_recv()
    own_a(unpack_u, unpack_f)
    for made in y_halo:
        made.wait_recv()
    halo_a(unpack_u, unpack_f, unpack_k)

    in_column = layers() < NZ
    beyond = ((lanes() < 64) & (ty == nty - 1)) | ((lanes() >= 64) & (ty == 0))
    inside = (in_column, in_column & jnp.logical_not(beyond))

    def row_inside(x, count):
        return jnp.logical_not(((x < 0) & (tx == 0)) | ((x >= count) & (tx == ntx - 1)))

    def fine_fields(x):
        for t in range(2):
            tile = cf[t, x + CO]
            keep = inside[t] & row_inside(x, LX)
            active = jnp.where(keep, jnp.broadcast_to(tile[6:7], (8, 128)), 0.0)
            a[t, x + FO] = active
            av[t, x + FO] = active * tile

    def coarse_fields(x):
        for t in range(2):
            tile = cf[t, 2 * x + CO] + cf[t, 2 * x + 1 + CO]
            other = jnp.where(lanes() % 2 == 0, pltpu.roll(tile, 127, 1), pltpu.roll(tile, 1, 1))
            tile = tile + other
            keep = inside[t] & row_inside(x, LX // 2)
            active = jnp.where(keep, 0.25 * jnp.broadcast_to(tile[6:7], (8, 128)), 0.0)
            kv[t, x + KO] = tile
            ka[t, x + KO] = active
            kav[t, x + KO] = active * tile

    def spread(field, low, high, spacing, shift, offset, flags, products):
        def body(x):
            r = x + offset
            for c in range(3):
                weight_y = 0.25 * spacing * (2.0 if c == 1 else 1.0)
                weight_z = 0.5 * (2.0 if c == 2 else 1.0)
                for k, scale in enumerate((flags, products)):
                    tiles = []
                    for t in range(2):
                        s = scale[t, r]
                        tiles.append(s if field is None else s * field[t, c, r])
                    tiles = along_y(tiles[0], tiles[1], weight_y, shift)
                    for t in range(2):
                        g[k, t, c, r] = along_z(tiles[t], weight_z)

        rows(low - 1, high + 1, 2, body)

    def coupled(t, c, r, spacing, flag, visc):
        weight = 0.25 * spacing * (2.0 if c == 0 else 1.0)
        p = g[0, t, c, r] + weight * (g[0, t, c, r - 1] + g[0, t, c, r + 1])
        q = g[1, t, c, r] + weight * (g[1, t, c, r - 1] + g[1, t, c, r + 1])
        return 2.0 * flag * (visc * p + q)

    def diagonals(low, high, spacing, ocean, shift, offset, flags, products, visc, diag, scaled):
        spread(None, low, high, spacing, shift, offset, flags, products)

        def body(x):
            r = x + offset
            for t in range(2):
                tile, flag, product = visc(t, x), flags[t, r], products[t, r]
                basal = jnp.where(layers() == 0, jnp.broadcast_to(tile[7:8], (8, 128)), 0.0)
                base = REACTION * product + ocean * (1.0 - flag)
                for c in range(3):
                    whole = coupled(t, c, r, spacing, flag, tile) + base
                    if c < 2:
                        whole = whole + basal
                    diag[t, c, r] = whole
                    scaled[t, c, r] = DAMPING / (whole - 4.0 * flag * product)

        rows(low, high, 2, body)

    def fine_visc(t, x):
        return cf[t, x + CO]

    def coarse_visc(t, x):
        return kv[t, x + KO]

    def fine_step(field, low, high, finish, tiles=(0, 1)):
        spread(field, low, high, 1.0, 1, FO, a, av)

        def body(x):
            r = x + FO
            for t in tiles:
                flag, visc = a[t, r], cf[t, x + CO]
                for c in range(3):
                    value = field[t, c, r]
                    left_over = f[t, c, r] - d[t, c, r] * value + coupled(t, c, r, 1.0, flag, visc)
                    finish(t, c, x, value, left_over)

        rows(low, high, 2, body)

    def smooth(field):
        def finish(t, c, x, value, left_over):
            field[t, c, x + FO] = value + inv[t, c, x + FO] * left_over

        return finish

    rows(-4, LX + 4, 4, fine_fields)
    diagonals(-2, LX + 2, 1.0, 1.0, 1, FO, a, av, fine_visc, d, inv)
    for made in x_a:
        made.wait_send()
    fine_step(u, -2, LX + 2, smooth(u))
    fine_step(u, -1, LX + 1, smooth(u))

    spread(u, 0, LX, 1.0, 1, FO, a, av)

    def restrict(X):
        for c in range(3):
            total = None
            for k in range(2):
                r = 2 * X + k + FO
                value = u[0, c, r]
                ub[0, c, r] = value
                part = coupled(0, c, r, 1.0, a[0, r], cf[0, 2 * X + k + CO])
                part = f[0, c, r] - d[0, c, r] * value + part
                total = part if total is None else total + part
            other = jnp.where(lanes() % 2 == 0, pltpu.roll(total, 127, 1), pltpu.roll(total, 1, 1))
            kr[0, c, X + KO] = total + other

    rows(0, LX // 2, 1, restrict)

    x_b = to_both_rows(tri(ub), FO, 3, LX)
    x_b += to_both_rows(tri(kr), KO, 5, LX // 2)

    def pack_b(ref, offset):
        def do(x, slot):
            pb[slot] = pack([ref[0, c, x + offset] for c in range(3)])

        return do

    def unpack_b(ref, offset):
        def do(x, slot):
            got = unpack(pbl[slot], pbr[slot], 3)
            for c in range(3):
                ref[1, c, x + offset] = got[c]

        return do

    def own_b(do_u, do_k):
        def body(X):
            do_u(2 * X, 2 * X)
            do_u(2 * X + 1, 2 * X + 1)
            do_k(X, LX + X)

        rows(0, LX // 2, 2, body)

    def halo_b(do_u, do_k):
        for j in range(3):
            do_u(j - 3, 24 + j)
            do_u(LX + j, 27 + j)
        for j in range(5):
            do_k(j - 5, 30 + j)
            do_k(LX // 2 + j, 35 + j)

    own_b(pack_b(ub, FO), pack_b(kr, KO))
    y_own_b = to_both_lanes(pb, pbl, pbr, 0, PACK_B_OWN)
    rows(-6, LX // 2 + 6, 4, coarse_fields)
    for made in x_b:
        made.wait_recv()
    halo_b(pack_b(ub, FO), pack_b(kr, KO))
    y_halo_b = to_both_lanes(pb, pbl, pbr, PACK_B_OWN, PACK_B - PACK_B_OWN)
    diagonals(-5, LX // 2 + 5, 0.5, 4.0, 2, KO, ka, kav, coarse_visc, kd, kinv)
    for made in y_own_b:
        made.wait_recv()
    own_b(unpack_b(ub, FO), unpack_b(kr, KO))
    for made in y_halo_b:
        made.wait_recv()
    halo_b(unpack_b(ub, FO), unpack_b(kr, KO))

    def first_coarse(x):
        for t in range(2):
            for c in range(3):
                kc[t, c, x + KO] = kinv[t, c, x + KO] * kr[t, c, x + KO]

    def coarse_step(low, high):
        spread(kc, low, high, 0.5, 2, KO, ka, kav)

        def body(x):
            r = x + KO
            for t in range(2):
                flag, visc = ka[t, r], kv[t, r]
                for c in range(3):
                    value = kc[t, c, r]
                    left_over = kr[t, c, r] - kd[t, c, r] * value
                    left_over = left_over + coupled(t, c, r, 0.5, flag, visc)
                    kc[t, c, r] = value + kinv[t, c, r] * left_over

        rows(low, high, 2, body)

    half = LX // 2
    rows(-5, half + 5, 3, first_coarse)
    coarse_step(-4, half + 4)
    coarse_step(-3, half + 3)
    coarse_step(-2, half + 2)

    def correct(X):
        for t in range(2):
            for c in range(3):
                step = kc[t, c, X + KO]
                for k in range(2):
                    ub[t, c, 2 * X + k + FO] = ub[t, c, 2 * X + k + FO] + step

    def correct_row(x, X):
        for t in range(2):
            for c in range(3):
                ub[t, c, x + FO] = ub[t, c, x + FO] + kc[t, c, X + KO]

    for made in x_b:
        made.wait_send()
    rows(-1, half + 1, 2, correct)
    correct_row(-3, -2)
    correct_row(LX + 2, half + 1)
    fine_step(ub, -2, LX + 2, smooth(ub))
    fine_step(ub, -1, LX + 1, smooth(ub))

    def finish(t, c, x, value, left_over):
        out_u[c, x] = value
        out_r[c, x] = left_over

    fine_step(ub, 0, LX, finish, (0,))

    for made in y_own + y_halo + y_own_b + y_halo_b:
        made.wait_send()


def shards(ntx, nty, forcing, start_state, ice_mask, class_ids, eta_table, friction):
    vmem = pl.BlockSpec(memory_space=pltpu.VMEM)

    def tiles(*lead):
        return pltpu.VMEM(lead + (8, 128), jnp.float32)

    out = jax.ShapeDtypeStruct((3, LX, 8, 128), jnp.float32)
    fine, coarse = tiles(2, 3, FROWS), tiles(2, 3, KROWS)
    adjoint, residual = pl.pallas_call(
        functools.partial(kernel, ntx, nty),
        out_shape=(out, out),
        in_specs=[pl.BlockSpec(memory_space=pltpu.SMEM)] + [vmem] * 5,
        out_specs=(vmem, vmem),
        scratch_shapes=[
            fine, fine, tiles(2, CROWS), tiles(2, FROWS), tiles(2, FROWS), fine, fine, fine,
            tiles(2, 2, 3, FROWS), tiles(2, KROWS), tiles(2, KROWS), tiles(2, KROWS),
            coarse, coarse, coarse, coarse,
            tiles(PACK_A), tiles(PACK_A), tiles(PACK_A),
            tiles(PACK_B), tiles(PACK_B), tiles(PACK_B),
            pltpu.SemaphoreType.DMA((18,)), pltpu.SemaphoreType.DMA((18,)),
        ],
        compiler_params=pltpu.CompilerParams(
            collective_id=0, has_side_effects=True, vmem_limit_bytes=32 * 1024 * 1024
        ),
    )(eta_table, forcing, start_state, ice_mask, class_ids, friction)

    def back(values):
        return jnp.transpose(values[:, :, :NZ], (0, 2, 1, 3))

    return back(adjoint), back(residual)


def solution(mesh):
    return jax.shard_map(
        functools.partial(shards, mesh.shape["tx"], mesh.shape["ty"]),
        mesh=mesh,
        in_specs=(
            P(None, None, "tx", "ty"),
            P(None, None, "tx", "ty"),
            P("tx", "ty"),
            P(None, "tx", "ty"),
            P(),
            P("tx", "ty"),
        ),
        out_specs=(P(None, None, "tx", "ty"), P(None, None, "tx", "ty")),
        check_vma=False,
    )
```

time: 268 us -> 54 us (0.20)
  the two profiles are of different devices: /device:TPU:22 before, /device:TPU:25 now
where the time goes in v1:
time: 54 us; the launch traced here: 53.7 us
  Pallas kernels  46.9 us (87%)
  local copies, waits for them, and re-layouts  6.06 us (11%)
  between operations  0.66 us (1%)
    pallas_call x1, Pallas kernels, shards(): pl.pallas_call(functools.partial(kernel, ntx, nty), out_shape=(out, out),...  46.9 us
    unnamed x14, local copies, waits for them, and re-layouts  6.03 us

profile of v1, /device:TPU:25, one launch (start us, length us, event | category | flops | bytes accessed | tf_op | source)
XLA Modules:
  0.0 53.7 jit_solution(13644732583155279765)
XLA Ops:
  0.6 0.0 copy-start
  0.6 0.9 %copy-done = f32[3,6,16,128]{3,2,1,0:T(8,128)S(1)} copy-done((f32[3,6,16,128]{3,2,1,0:T(8,128)S(1)}, f32[3,6,16,128]{3,2,1,0:T(8,128)}, u32[]{:S(2)}) %copy-start) | copy-done | bytes 147480
  1.5 0.0 copy-start.1
  1.5 0.9 %copy-done.1 = f32[3,6,16,128]{3,2,1,0:T(8,128)S(1)} copy-done((f32[3,6,16,128]{3,2,1,0:T(8,128)S(1)}, f32[3,6,16,128]{3,2,1,0:T(8,128)}, u32[]{:S(2)}) %copy-start.1) | copy-done | bytes 147480
  2.5 0.0 copy-start.2
  2.5 0.8 %copy-done.2 = s32[6,16,128]{2,1,0:T(8,128)S(1)} copy-done((s32[6,16,128]{2,1,0:T(8,128)S(1)}, s32[6,16,128]{2,1,0:T(8,128)}, u32[]{:S(2)}) %copy-start.2) | copy-done | bytes 49176
  3.3 0.0 copy-start.3
  3.3 0.7 %copy-done.3 = s32[16,128]{1,0:T(8,128)S(1)} copy-done((s32[16,128]{1,0:T(8,128)S(1)}, s32[16,128]{1,0:T(8,128)}, u32[]{:S(2)}) %copy-start.3) | copy-done | bytes 8216
  3.9 0.0 copy-start.4
  4.0 0.7 %copy-done.4 = f32[16,128]{1,0:T(8,128)S(1)} copy-done((f32[16,128]{1,0:T(8,128)S(1)}, f32[16,128]{1,0:T(8,128)}, u32[]{:S(2)}) %copy-start.4) | copy-done | bytes 8216
  4.6 0.0 copy-start.5
  4.6 0.7 %copy-done.5 = f32[16]{0:T(128)S(1)} copy-done((f32[16]{0:T(128)S(1)}, f32[16]{0:T(128)}, u32[]{:S(2)}) %copy-start.5) | copy-done | bytes 88
  5.3 46.9 %shard_map.77 = (f32[3,16,8,128]{3,2,1,0:T(8,128)S(1)}, f32[3,16,8,128]{3,2,1,0:T(8,128)S(1)}) custom-call(f32[16]{0:T(128)S(1)} %copy-done.5, f32[3,6,16,128]{3,2,1,0:T(8,128)S(1)} %copy-done, f32[3,6,16,128]{3,2,1,0:T(8,128)S(1)} %copy-done.1, s32[16,128]{1,0:T(8,128)S(1)} %copy-done.3, s32[6,16,128]{2,1,0:T(8,128)S(1)} %copy-done.2, f32[16,128]{1,0:T(8,128)S(1)} %copy-done.4), custom_call_target="tpu_custom_call" | custom-call | tf_op jit(solution)/shard_map/pallas_call | solution.py:410
  52.3 0.7 %copy.9 = f32[3,6,16,128]{3,2,1,0:T(8,128)} copy(f32[3,6,16,128]{3,1,2,0:T(8,128)S(1)} %get-tuple-element.8) | data formatting | bytes 294912
  53.0 0.7 %copy.8 = f32[3,6,16,128]{3,2,1,0:T(8,128)} copy(f32[3,6,16,128]{3,1,2,0:T(8,128)S(1)} %get-tuple-element.9) | data formatting | bytes 294912
  (1 shorter events, 0.0 us)
Async XLA Ops:
  0.6 0.9 %copy-start = (f32[3,6,16,128]{3,2,1,0:T(8,128)S(1)}, f32[3,6,16,128]{3,2,1,0:T(8,128)}, u32[]{:S(2)}) copy-start(f32[3,6,16,128]{3,2,1,0:T(8,128)} %forcing.1) | copy-start | bytes 442372
  1.5 0.9 %copy-start.1 = (f32[3,6,16,128]{3,2,1,0:T(8,128)S(1)}, f32[3,6,16,128]{3,2,1,0:T(8,128)}, u32[]{:S(2)}) copy-start(f32[3,6,16,128]{3,2,1,0:T(8,128)} %start.1) | copy-start | bytes 442372
  2.5 0.8 %copy-start.2 = (s32[6,16,128]{2,1,0:T(8,128)S(1)}, s32[6,16,128]{2,1,0:T(8,128)}, u32[]{:S(2)}) copy-start(s32[6,16,128]{2,1,0:T(8,128)} %classes.1) | copy-start | bytes 147460
  3.3 0.7 %copy-start.3 = (s32[16,128]{1,0:T(8,128)S(1)}, s32[16,128]{1,0:T(8,128)}, u32[]{:S(2)}) copy-start(s32[16,128]{1,0:T(8,128)} %mask.1) | copy-start | bytes 24580
  3.9 0.7 %copy-start.4 = (f32[16,128]{1,0:T(8,128)S(1)}, f32[16,128]{1,0:T(8,128)}, u32[]{:S(2)}) copy-start(f32[16,128]{1,0:T(8,128)} %friction.1) | copy-start | bytes 24580
  4.6 0.7 %copy-start.5 = (f32[16]{0:T(128)S(1)}, f32[16]{0:T(128)}, u32[]{:S(2)}) copy-start(f32[16]{0:T(128)} %eta.1) | copy-start | bytes 196

commit v2 on v1

v2 whole, which is shorter than its diff:
```python
import functools

import jax
import jax.numpy as jnp
from jax import lax
from jax.experimental import pallas as pl
from jax.experimental.pallas import tpu as pltpu
from jax.sharding import PartitionSpec as P

DAMPING = 0.6
REACTION = 0.05
NZ = 6
LX = 16
FO = 4
CO = 12
KO = 6
FROWS = LX + 2 * FO
CROWS = LX + 2 * CO
KROWS = LX // 2 + 2 * KO
PACK_A_OWN, PACK_A = 32, 48
PACK_B_OWN, PACK_B = 24, 40


def lanes():
    return lax.broadcasted_iota(jnp.int32, (8, 128), 1)


def layers():
    return lax.broadcasted_iota(jnp.int32, (8, 128), 0)


def rows(low, high, body):
    step = next(k for k in (4, 3, 2) if (high - low) % k == 0)

    def run(i, carry):
        for k in range(step):
            body(low + i * step + k)
        return carry

    lax.fori_loop(0, (high - low) // step, run, 0)


def along_y(tiles, weights, shift, edges):
    mains, halo = tiles[:3], tiles[3]
    lane = lanes()
    out = []
    for c in range(3):
        near = pltpu.roll(halo, 112 - 32 * c, 1)
        below = pltpu.roll(jnp.where(lane >= 128 - shift, near, mains[c]), shift, 1)
        above = pltpu.roll(jnp.where(lane < shift, near, mains[c]), 128 - shift, 1)
        out.append(mains[c] + weights[c] * (below + above))
    if edges:
        near, place = pack(mains), lane % 32
        below = pltpu.roll(jnp.where((place >= 16 - shift) & (place < 16), near, halo), shift, 1)
        above = pltpu.roll(
            jnp.where((place >= 16) & (place < 16 + shift), near, halo), 128 - shift, 1
        )
        out.append(halo + weights[3] * (below + above))
    return out


def factors(base, doubled):
    each = [base * (2.0 if c == doubled else 1.0) for c in range(3)]
    packed = jnp.where(lanes() // 32 == doubled, 2.0 * base, base).astype(jnp.float32)
    return each + [packed]


def along_z(tile, weight):
    return tile + weight * (pltpu.roll(tile, 1, 0) + pltpu.roll(tile, 7, 0))


def pack(items):
    packed = pltpu.roll(items[0], 16, 1)
    for j in range(1, len(items)):
        packed = jnp.where(lanes() >= 32 * j, pltpu.roll(items[j], 16 + 32 * j, 1), packed)
    return packed


def edges_of(from_left, from_right):
    return jnp.where(lanes() % 32 < 16, from_left, from_right)


def repeated(packed, j):
    out = packed if j == 0 else pltpu.roll(packed, 128 - 32 * j, 1)
    for c in (1, 2):
        moved = pltpu.roll(packed, (32 * (c - j)) % 128, 1) if c != j else packed
        out = jnp.where(lanes() >= 32 * c, moved, out)
    return out


def kernel(
    ntx, nty,
    eta, forcing, start, mask, classes, friction, out_u, out_r,
    u, f, cf, a, av, d, inv, ub, g, ka, kav, kv, kd, kinv, kr, kc,
    pa, pal, par, pb, pbl, pbr, in_start, in_forcing, in_classes, in_mask, in_friction, send, recv, load,
):
    tx, ty = lax.axis_index("tx"), lax.axis_index("ty")
    up, down = lax.rem(tx + 1, ntx), lax.rem(tx + ntx - 1, ntx)
    right, left = lax.rem(ty + 1, nty), lax.rem(ty + nty - 1, nty)
    pairs = ((classes, in_classes), (mask, in_mask), (friction, in_friction),
             (start, in_start), (forcing, in_forcing))
    loads = [pltpu.make_async_copy(src, dst, load.at[k]) for k, (src, dst) in enumerate(pairs)]
    for made in loads:
        made.start()
    barrier = pltpu.get_barrier_semaphore()
    for where in ({"tx": up}, {"tx": down}, {"ty": right}, {"ty": left}):
        pl.semaphore_signal(barrier, inc=1, device_id=where, device_id_type=pl.DeviceIdType.MESH)

    zero = jnp.zeros((LX, 128), jnp.float32)
    for c in range(3):
        for z in range(NZ, 8):
            u[c, FO : FO + LX, z, :] = zero
            f[c, FO : FO + LX, z, :] = zero
    for made in loads[:3]:
        made.wait()
    for z in range(NZ):
        ids = in_classes[z]
        visc = jnp.zeros((LX, 128), jnp.float32)
        for k in range(eta.shape[0]):
            visc = jnp.where(ids == k, eta[k], visc)
        cf[0, CO : CO + LX, z, :] = visc
    kind = in_mask[...]
    cf[0, CO : CO + LX, 6, :] = jnp.where(kind != 0, 1.0, 0.0).astype(jnp.float32)
    cf[0, CO : CO + LX, 7, :] = jnp.where(kind == 1, in_friction[...], 0.0)

    used = [0]

    def copy(src, dst, where):
        k = used[0]
        used[0] += 1
        made = pltpu.make_async_remote_copy(
            src_ref=src, dst_ref=dst, send_sem=send.at[k], recv_sem=recv.at[k],
            device_id=where, device_id_type=pl.DeviceIdType.MESH,
        )
        made.start()
        return made

    def to_both_rows(make, first, count, own):
        top = copy(make(first + own - count, count), make(first - count, count), {"tx": up})
        low = copy(make(first, count), make(first + own, count), {"tx": down})
        return [top, low]

    def to_both_lanes(packed, from_left, from_right, first, count):
        part = pl.ds(first, count)
        return [
            copy(packed.at[part], from_left.at[part], {"ty": right}),
            copy(packed.at[part], from_right.at[part], {"ty": left}),
        ]

    def tri(ref):
        return lambda first, count: ref.at[pl.ds(0, 3), pl.ds(first, count)]

    pl.semaphore_wait(barrier, 4)
    x_a = to_both_rows(lambda first, count: cf.at[0, pl.ds(first, count)], CO, 12, LX)
    for made, ref, src in ((loads[3], u, in_start), (loads[4], f, in_forcing)):
        made.wait()
        for c in range(3):
            for z in range(NZ):
                ref[c, FO : FO + LX, z, :] = src[c, z]
        x_a += to_both_rows(tri(ref), FO, 4 if ref is u else 2, LX)

    def pack_u(x, slot):
        pa[slot] = pack([u[c, x + FO] for c in range(3)] + [cf[0, x + CO]])

    def pack_f(x, slot):
        pa[slot] = pack([f[c, x + FO] for c in range(3)])

    def pack_k(x, slot):
        pa[slot] = pack([cf[0, x + CO + j] for j in range(4)])

    def unpack_u(x, slot):
        both = edges_of(pal[slot], par[slot])
        u[3, x + FO] = both
        cf[1, x + CO] = repeated(both, 3)

    def unpack_f(x, slot):
        f[3, x + FO] = edges_of(pal[slot], par[slot])

    def unpack_k(x, slot):
        both = edges_of(pal[slot], par[slot])
        for j in range(4):
            cf[1, x + CO + j] = repeated(both, j)

    def own_a(do_u, do_f):
        def body(x):
            do_u(x, x)
            do_f(x, x + LX)

        rows(0, LX, body)

    def halo_a(do_u, do_f, do_k):
        for j in range(4):
            do_u(j - 4, 32 + j)
            do_u(LX + j, 36 + j)
        for j in range(2):
            do_f(j - 2, 40 + j)
            do_f(LX + j, 42 + j)
            do_k(4 * j - 12, 44 + j)
            do_k(LX + 4 + 4 * j, 46 + j)

    own_a(pack_u, pack_f)
    y_own = to_both_lanes(pa, pal, par, 0, PACK_A_OWN)
    for made in x_a:
        made.wait_recv()
    halo_a(pack_u, pack_f, pack_k)
    y_halo = to_both_lanes(pa, pal, par, PACK_A_OWN, PACK_A - PACK_A_OWN)
    for made in y_own:
        made.wait_recv()
    own_a(unpack_u, unpack_f)
    for made in y_halo:
        made.wait_recv()
    halo_a(unpack_u, unpack_f, unpack_k)

    in_column = layers() < NZ
    beyond = ((lanes() % 32 >= 16) & (ty == nty - 1)) | ((lanes() % 32 < 16) & (ty == 0))
    inside = (in_column, in_column & jnp.logical_not(beyond))

    def row_inside(x, count):
        return jnp.logical_not(((x < 0) & (tx == 0)) | ((x >= count) & (tx == ntx - 1)))

    def fine_fields(x):
        for t in range(2):
            tile = cf[t, x + CO]
            keep = inside[t] & row_inside(x, LX)
            active = jnp.where(keep, jnp.broadcast_to(tile[6:7], (8, 128)), 0.0)
            a[t, x + FO] = active
            av[t, x + FO] = active * tile

    def coarse_fields(x):
        for t in range(2):
            tile = cf[t, 2 * x + CO] + cf[t, 2 * x + 1 + CO]
            other = jnp.where(lanes() % 2 == 0, pltpu.roll(tile, 127, 1), pltpu.roll(tile, 1, 1))
            tile = tile + other
            keep = inside[t] & row_inside(x, LX // 2)
            active = jnp.where(keep, 0.25 * jnp.broadcast_to(tile[6:7], (8, 128)), 0.0)
            kv[t, x + KO] = tile
            ka[t, x + KO] = active
            kav[t, x + KO] = active * tile

    def spread(field, low, high, spacing, shift, offset, flags, products, edges=True):
        weights_y, weights_z = factors(0.25 * spacing, 1), factors(0.5, 2)

        def body(x):
            r = x + offset
            for k, scale in enumerate((flags, products)):
                own, beside = scale[0, r], scale[1, r]
                tiles = [own] * 3 + [beside]
                if field is not None:
                    tiles = [tiles[c] * field[c, r] for c in range(4)]
                for c, tile in enumerate(along_y(tiles, weights_y, shift, edges)):
                    g[k, c, r] = along_z(tile, weights_z[c])

        rows(low - 1, high + 1, body)

    def coupled(c, r, weights_x, flag, visc):
        p = g[0, c, r] + weights_x[c] * (g[0, c, r - 1] + g[0, c, r + 1])
        q = g[1, c, r] + weights_x[c] * (g[1, c, r - 1] + g[1, c, r + 1])
        return 2.0 * flag * (visc * p + q)

    def diagonals(low, high, spacing, ocean, shift, offset, flags, products, visc, diag, scaled):
        spread(None, low, high, spacing, shift, offset, flags, products)
        weights_x = factors(0.25 * spacing, 0)

        def body(x):
            r = x + offset
            for t in range(2):
                tile, flag, product = visc(t, x), flags[t, r], products[t, r]
                bottom = layers() == 0
                if t == 1:
                    bottom = bottom & (lanes() < 64)
                basal = jnp.where(bottom, jnp.broadcast_to(tile[7:8], (8, 128)), 0.0)
                base = REACTION * product + ocean * (1.0 - flag)
                for c in (3,) if t == 1 else range(3):
                    whole = coupled(c, r, weights_x, flag, tile) + base
                    if c != 2:
                        whole = whole + basal
                    diag[c, r] = whole
                    scaled[c, r] = DAMPING / (whole - 4.0 * flag * product)

        rows(low, high, body)

    def fine_visc(t, x):
        return cf[t, x + CO]

    def coarse_visc(t, x):
        return kv[t, x + KO]

    def fine_step(field, low, high, finish, edges=True):
        spread(field, low, high, 1.0, 1, FO, a, av, edges)
        weights_x = factors(0.25, 0)

        def body(x):
            r = x + FO
            for c in range(4 if edges else 3):
                flag, visc = a[c // 3, r], cf[c // 3, x + CO]
                value = field[c, r]
                left_over = f[c, r] - d[c, r] * value + coupled(c, r, weights_x, flag, visc)
                finish(c, x, value, left_over)

        rows(low, high, body)

    def smooth(field):
        def finish(c, x, value, left_over):
            field[c, x + FO] = value + inv[c, x + FO] * left_over

        return finish

    rows(-4, LX + 4, fine_fields)
    diagonals(-2, LX + 2, 1.0, 1.0, 1, FO, a, av, fine_visc, d, inv)
    for made in x_a:
        made.wait_send()
    fine_step(u, -2, LX + 2, smooth(u))
    fine_step(u, -1, LX + 1, smooth(u))

    spread(u, 0, LX, 1.0, 1, FO, a, av, False)
    fine_x = factors(0.25, 0)

    def restrict(X):
        for c in range(3):
            total = None
            for k in range(2):
                r = 2 * X + k + FO
                value = u[c, r]
                ub[c, r] = value
                part = coupled(c, r, fine_x, a[0, r], cf[0, 2 * X + k + CO])
                part = f[c, r] - d[c, r] * value + part
                total = part if total is None else total + part
            other = jnp.where(lanes() % 2 == 0, pltpu.roll(total, 127, 1), pltpu.roll(total, 1, 1))
            kr[c, X + KO] = total + other

    rows(0, LX // 2, restrict)

    x_b = to_both_rows(tri(ub), FO, 3, LX)
    x_b += to_both_rows(tri(kr), KO, 5, LX // 2)

    def pack_b(ref, offset):
        def do(x, slot):
            pb[slot] = pack([ref[c, x + offset] for c in range(3)])

        return do

    def unpack_b(ref, offset):
        def do(x, slot):
            ref[3, x + offset] = edges_of(pbl[slot], pbr[slot])

        return do

    def own_b(do_u, do_k):
        def body(X):
            do_u(2 * X, 2 * X)
            do_u(2 * X + 1, 2 * X + 1)
            do_k(X, LX + X)

        rows(0, LX // 2, body)

    def halo_b(do_u, do_k):
        for j in range(3):
            do_u(j - 3, 24 + j)
            do_u(LX + j, 27 + j)
        for j in range(5):
            do_k(j - 5, 30 + j)
            do_k(LX // 2 + j, 35 + j)

    own_b(pack_b(ub, FO), pack_b(kr, KO))
    y_own_b = to_both_lanes(pb, pbl, pbr, 0, PACK_B_OWN)
    rows(-6, LX // 2 + 6, coarse_fields)
    for made in x_b:
        made.wait_recv()
    halo_b(pack_b(ub, FO), pack_b(kr, KO))
    y_halo_b = to_both_lanes(pb, pbl, pbr, PACK_B_OWN, PACK_B - PACK_B_OWN)
    diagonals(-5, LX // 2 + 5, 0.5, 4.0, 2, KO, ka, kav, coarse_visc, kd, kinv)
    for made in y_own_b:
        made.wait_recv()
    own_b(unpack_b(ub, FO), unpack_b(kr, KO))
    for made in y_halo_b:
        made.wait_recv()
    halo_b(unpack_b(ub, FO), unpack_b(kr, KO))

    def first_coarse(x):
        for c in range(4):
            kc[c, x + KO] = kinv[c, x + KO] * kr[c, x + KO]

    def coarse_step(low, high):
        spread(kc, low, high, 0.5, 2, KO, ka, kav)
        weights_x = factors(0.125, 0)

        def body(x):
            r = x + KO
            for c in range(4):
                flag, visc = ka[c // 3, r], kv[c // 3, r]
                value = kc[c, r]
                left_over = kr[c, r] - kd[c, r] * value
                left_over = left_over + coupled(c, r, weights_x, flag, visc)
                kc[c, r] = value + kinv[c, r] * left_over

        rows(low, high, body)

    half = LX // 2
    rows(-5, half + 5, first_coarse)
    coarse_step(-4, half + 4)
    coarse_step(-3, half + 3)
    coarse_step(-2, half + 2)

    def correct_row(x, X):
        for c in range(4):
            ub[c, x + FO] = ub[c, x + FO] + kc[c, X + KO]

    def correct(X):
        correct_row(2 * X, X)
        correct_row(2 * X + 1, X)

    for made in x_b:
        made.wait_send()
    rows(-1, half + 1, correct)
    correct_row(-3, -2)
    correct_row(LX + 2, half + 1)
    fine_step(ub, -2, LX + 2, smooth(ub))
    fine_step(ub, -1, LX + 1, smooth(ub))

    def finish(c, x, value, left_over):
        out_u[c, x] = value
        out_r[c, x] = left_over

    fine_step(ub, 0, LX, finish, False)

    for made in y_own + y_halo + y_own_b + y_halo_b:
        made.wait_send()


def shards(ntx, nty, forcing, start_state, ice_mask, class_ids, eta_table, friction):
    vmem = pl.BlockSpec(memory_space=pltpu.VMEM)

    def tiles(*lead):
        return pltpu.VMEM(lead + (8, 128), jnp.float32)

    out = jax.ShapeDtypeStruct((3, LX, 8, 128), jnp.float32)
    fine, coarse = tiles(4, FROWS), tiles(4, KROWS)
    hbm = pl.BlockSpec(memory_space=pltpu.HBM)
    adjoint, residual = pl.pallas_call(
        functools.partial(kernel, ntx, nty),
        out_shape=(out, out),
        in_specs=[pl.BlockSpec(memory_space=pltpu.SMEM)] + [hbm] * 5,
        out_specs=(vmem, vmem),
        scratch_shapes=[
            fine, fine, tiles(2, CROWS), tiles(2, FROWS), tiles(2, FROWS), fine, fine, fine,
            tiles(2, 4, FROWS), tiles(2, KROWS), tiles(2, KROWS), tiles(2, KROWS),
            coarse, coarse, coarse, coarse,
            tiles(PACK_A), tiles(PACK_A), tiles(PACK_A),
            tiles(PACK_B), tiles(PACK_B), tiles(PACK_B),
            pltpu.VMEM((3, NZ, LX, 128), jnp.float32), pltpu.VMEM((3, NZ, LX, 128), jnp.float32),
            pltpu.VMEM((NZ, LX, 128), jnp.int32), pltpu.VMEM((LX, 128), jnp.int32),
            pltpu.VMEM((LX, 128), jnp.float32),
            pltpu.SemaphoreType.DMA((18,)), pltpu.SemaphoreType.DMA((18,)), pltpu.SemaphoreType.DMA((5,)),
        ],
        compiler_params=pltpu.CompilerParams(
            collective_id=0, has_side_effects=True, vmem_limit_bytes=32 * 1024 * 1024
        ),
    )(eta_table, forcing, start_state, ice_mask, class_ids, friction)

    def back(values):
        return jnp.transpose(values[:, :, :NZ], (0, 2, 1, 3))

    return back(adjoint), back(residual)


def solution(mesh):
    return jax.shard_map(
        functools.partial(shards, mesh.shape["tx"], mesh.shape["ty"]),
        mesh=mesh,
        in_specs=(
            P(None, None, "tx", "ty"),
            P(None, None, "tx", "ty"),
            P("tx", "ty"),
            P(None, "tx", "ty"),
            P(),
            P("tx", "ty"),
        ),
        out_specs=(P(None, None, "tx", "ty"), P(None, None, "tx", "ty")),
        check_vma=False,
    )
```

time: 54 us -> 54.9 us (1.017)
  Pallas kernels: 46.9 us -> 47.9 us
    pallas_call x1, Pallas kernels: 46.9 us -> 47.9 us  [shards(): pl.pallas_call(functools.partial(kernel, ntx, nty), out_shape=(out, out),...]
where the time goes in v2:
time: 54.9 us; the launch traced here: 54.6 us
  Pallas kernels  47.9 us (87%)
  local copies, waits for them, and re-layouts  6.06 us (11%)
  between operations  0.66 us (1%)
    pallas_call x1, Pallas kernels, shards(): pl.pallas_call(functools.partial(kernel, ntx, nty), out_shape=(out, out),...  47.9 us
    unnamed x14, local copies, waits for them, and re-layouts  6.03 us

profile of v2, /device:TPU:25, one launch (start us, length us, event | category | flops | bytes accessed | tf_op | source)
XLA Modules:
  0.0 54.6 jit_solution(6320427185996524591)
XLA Ops:
  0.6 0.0 copy-start
  0.6 0.9 %copy-done = f32[3,6,16,128]{3,2,1,0:T(8,128)S(1)} copy-done((f32[3,6,16,128]{3,2,1,0:T(8,128)S(1)}, f32[3,6,16,128]{3,2,1,0:T(8,128)}, u32[]{:S(2)}) %copy-start) | copy-done | bytes 147480
  1.5 0.0 copy-start.1
  1.5 0.9 %copy-done.1 = f32[3,6,16,128]{3,2,1,0:T(8,128)S(1)} copy-done((f32[3,6,16,128]{3,2,1,0:T(8,128)S(1)}, f32[3,6,16,128]{3,2,1,0:T(8,128)}, u32[]{:S(2)}) %copy-start.1) | copy-done | bytes 147480
  2.5 0.0 copy-start.2
  2.5 0.8 %copy-done.2 = s32[6,16,128]{2,1,0:T(8,128)S(1)} copy-done((s32[6,16,128]{2,1,0:T(8,128)S(1)}, s32[6,16,128]{2,1,0:T(8,128)}, u32[]{:S(2)}) %copy-start.2) | copy-done | bytes 49176
  3.3 0.0 copy-start.3
  3.3 0.7 %copy-done.3 = s32[16,128]{1,0:T(8,128)S(1)} copy-done((s32[16,128]{1,0:T(8,128)S(1)}, s32[16,128]{1,0:T(8,128)}, u32[]{:S(2)}) %copy-start.3) | copy-done | bytes 8216
  3.9 0.0 copy-start.4
  4.0 0.7 %copy-done.4 = f32[16,128]{1,0:T(8,128)S(1)} copy-done((f32[16,128]{1,0:T(8,128)S(1)}, f32[16,128]{1,0:T(8,128)}, u32[]{:S(2)}) %copy-start.4) | copy-done | bytes 8216
  4.6 0.0 copy-start.5
  4.6 0.7 %copy-done.5 = f32[16]{0:T(128)S(1)} copy-done((f32[16]{0:T(128)S(1)}, f32[16]{0:T(128)}, u32[]{:S(2)}) %copy-start.5) | copy-done | bytes 88
  5.3 47.9 %shard_map.77 = (f32[3,16,8,128]{3,2,1,0:T(8,128)S(1)}, f32[3,16,8,128]{3,2,1,0:T(8,128)S(1)}) custom-call(f32[16]{0:T(128)S(1)} %copy-done.5, f32[3,6,16,128]{3,2,1,0:T(8,128)S(1)} %copy-done, f32[3,6,16,128]{3,2,1,0:T(8,128)S(1)} %copy-done.1, s32[16,128]{1,0:T(8,128)S(1)} %copy-done.3, s32[6,16,128]{2,1,0:T(8,128)S(1)} %copy-done.2, f32[16,128]{1,0:T(8,128)S(1)} %copy-done.4), custom_call_target="tpu_custom_call" | custom-call | tf_op jit(solution)/shard_map/pallas_call | solution.py:439
  53.2 0.7 %copy.9 = f32[3,6,16,128]{3,2,1,0:T(8,128)} copy(f32[3,6,16,128]{3,1,2,0:T(8,128)S(1)} %get-tuple-element.8) | data formatting | bytes 294912
  53.9 0.7 %copy.8 = f32[3,6,16,128]{3,2,1,0:T(8,128)} copy(f32[3,6,16,128]{3,1,2,0:T(8,128)S(1)} %get-tuple-element.9) | data formatting | bytes 294912
  (1 shorter events, 0.0 us)
Async XLA Ops:
  0.6 0.9 %copy-start = (f32[3,6,16,128]{3,2,1,0:T(8,128)S(1)}, f32[3,6,16,128]{3,2,1,0:T(8,128)}, u32[]{:S(2)}) copy-start(f32[3,6,16,128]{3,2,1,0:T(8,128)} %forcing.1) | copy-start | bytes 442372
  1.5 0.9 %copy-start.1 = (f32[3,6,16,128]{3,2,1,0:T(8,128)S(1)}, f32[3,6,16,128]{3,2,1,0:T(8,128)}, u32[]{:S(2)}) copy-start(f32[3,6,16,128]{3,2,1,0:T(8,128)} %start.1) | copy-start | bytes 442372
  2.5 0.8 %copy-start.2 = (s32[6,16,128]{2,1,0:T(8,128)S(1)}, s32[6,16,128]{2,1,0:T(8,128)}, u32[]{:S(2)}) copy-start(s32[6,16,128]{2,1,0:T(8,128)} %classes.1) | copy-start | bytes 147460
  3.3 0.7 %copy-start.3 = (s32[16,128]{1,0:T(8,128)S(1)}, s32[16,128]{1,0:T(8,128)}, u32[]{:S(2)}) copy-start(s32[16,128]{1,0:T(8,128)} %mask.1) | copy-start | bytes 24580
  3.9 0.7 %copy-start.4 = (f32[16,128]{1,0:T(8,128)S(1)}, f32[16,128]{1,0:T(8,128)}, u32[]{:S(2)}) copy-start(f32[16,128]{1,0:T(8,128)} %friction.1) | copy-start | bytes 24580
  4.6 0.7 %copy-start.5 = (f32[16]{0:T(128)S(1)}, f32[16]{0:T(128)}, u32[]{:S(2)}) copy-start(f32[16]{0:T(128)} %eta.1) | copy-start | bytes 196

commit v3 on v2

--- a/solution.py
+++ b/solution.py
@@ -90,15 +90,15 @@
 
 def kernel(
     ntx, nty,
-    eta, forcing, start, mask, classes, friction, out_u, out_r,
+    table, forcing, start, mask, classes, friction, out_u, out_r,
     u, f, cf, a, av, d, inv, ub, g, ka, kav, kv, kd, kinv, kr, kc,
-    pa, pal, par, pb, pbl, pbr, in_start, in_forcing, in_classes, in_mask, in_friction, send, recv, load,
+    pa, pal, par, pb, pbl, pbr, in_start, in_forcing, in_classes, in_mask, in_friction, eta, send, recv, load,
 ):
     tx, ty = lax.axis_index("tx"), lax.axis_index("ty")
     up, down = lax.rem(tx + 1, ntx), lax.rem(tx + ntx - 1, ntx)
     right, left = lax.rem(ty + 1, nty), lax.rem(ty + nty - 1, nty)
     pairs = ((classes, in_classes), (mask, in_mask), (friction, in_friction),
-             (start, in_start), (forcing, in_forcing))
+             (table, eta), (start, in_start), (forcing, in_forcing))
     loads = [pltpu.make_async_copy(src, dst, load.at[k]) for k, (src, dst) in enumerate(pairs)]
     for made in loads:
         made.start()
@@ -111,7 +111,7 @@
         for z in range(NZ, 8):
             u[c, FO : FO + LX, z, :] = zero
             f[c, FO : FO + LX, z, :] = zero
-    for made in loads[:3]:
+    for made in loads[:4]:
         made.wait()
     for z in range(NZ):
         ids = in_classes[z]
@@ -152,7 +152,7 @@
 
     pl.semaphore_wait(barrier, 4)
     x_a = to_both_rows(lambda first, count: cf.at[0, pl.ds(first, count)], CO, 12, LX)
-    for made, ref, src in ((loads[3], u, in_start), (loads[4], f, in_forcing)):
+    for made, ref, src in ((loads[4], u, in_start), (loads[5], f, in_forcing)):
         made.wait()
         for c in range(3):
             for z in range(NZ):
@@ -439,7 +439,7 @@
     adjoint, residual = pl.pallas_call(
         functools.partial(kernel, ntx, nty),
         out_shape=(out, out),
-        in_specs=[pl.BlockSpec(memory_space=pltpu.SMEM)] + [hbm] * 5,
+        in_specs=[hbm] * 6,
         out_specs=(vmem, vmem),
         scratch_shapes=[
             fine, fine, tiles(2, CROWS), tiles(2, FROWS), tiles(2, FROWS), fine, fine, fine,
@@ -449,13 +449,16 @@
             tiles(PACK_B), tiles(PACK_B), tiles(PACK_B),
             pltpu.VMEM((3, NZ, LX, 128), jnp.float32), pltpu.VMEM((3, NZ, LX, 128), jnp.float32),
             pltpu.VMEM((NZ, LX, 128), jnp.int32), pltpu.VMEM((LX, 128), jnp.int32),
-            pltpu.VMEM((LX, 128), jnp.float32),
-            pltpu.SemaphoreType.DMA((18,)), pltpu.SemaphoreType.DMA((18,)), pltpu.SemaphoreType.DMA((5,)),
+            pltpu.VMEM((LX, 128), jnp.float32), pltpu.SMEM((16,), jnp.float32),
+            pltpu.SemaphoreType.DMA((18,)), pltpu.SemaphoreType.DMA((18,)), pltpu.SemaphoreType.DMA((6,)),
         ],
         compiler_params=pltpu.CompilerParams(
-            collective_id=0, has_side_effects=True, vmem_limit_bytes=32 * 1024 * 1024
+            collective_id=0, has_side_effects=True, vmem_limit_bytes=32 << 20
         ),
-    )(eta_table, forcing, start_state, ice_mask, class_ids, friction)
+    )(*(
+        pltpu.with_memory_space_constraint(value, pltpu.HBM)
+        for value in (eta_table, forcing, start_state, ice_mask, class_ids, friction)
+    ))
 
     def back(values):
         return jnp.transpose(values[:, :, :NZ], (0, 2, 1, 3))

time: 54.9 us -> 49.1 us (0.89)
  local copies, waits for them, and re-layouts: 6.06 us -> 1.4 us
  Pallas kernels: 47.9 us -> 46.9 us
    unnamed x14 -> x2, local copies, waits for them, and re-layouts: 6.03 us -> 1.38 us
    pallas_call x1, Pallas kernels: 47.9 us -> 46.9 us  [shards(): pl.pallas_call(functools.partial(kernel, ntx, nty), out_shape=(out, out),...]
where the time goes in v3:
time: 49.1 us; the launch traced here: 48.9 us
  Pallas kernels  46.9 us (96%)
  local copies, waits for them, and re-layouts  1.4 us (3%)
  between operations  0.65 us (1%)
    pallas_call x1, Pallas kernels, shards(): pl.pallas_call(functools.partial(kernel, ntx, nty), out_shape=(out, out),...  46.9 us
    unnamed x2, local copies, waits for them, and re-layouts  1.38 us

profile of v3, /device:TPU:25, one launch (start us, length us, event | category | flops | bytes accessed | tf_op | source)
XLA Modules:
  0.0 48.9 jit_solution(11573359727591449740)
XLA Ops:
  0.6 46.9 %shard_map.77 = (f32[3,16,8,128]{3,2,1,0:T(8,128)S(1)}, f32[3,16,8,128]{3,2,1,0:T(8,128)S(1)}) custom-call(f32[16]{0:T(128)} %table.1, f32[3,6,16,128]{3,2,1,0:T(8,128)} %forcing.1, f32[3,6,16,128]{3,2,1,0:T(8,128)} %start.1, s32[16,128]{1,0:T(8,128)} %mask.1, s32[6,16,128]{2,1,0:T(8,128)} %classes.1, f32[16,128]{1,0:T(8,128)} %friction.1), custom_call_target="tpu_custom_call" | custom-call | tf_op jit(solution)/shard_map/pallas_call | solution.py:439
  47.6 0.7 %copy.9 = f32[3,6,16,128]{3,2,1,0:T(8,128)} copy(f32[3,6,16,128]{3,1,2,0:T(8,128)S(1)} %get-tuple-element.8) | data formatting | bytes 294912
  48.2 0.7 %copy.8 = f32[3,6,16,128]{3,2,1,0:T(8,128)} copy(f32[3,6,16,128]{3,1,2,0:T(8,128)S(1)} %get-tuple-element.9) | data formatting | bytes 294912
  (1 shorter events, 0.0 us)

commit v4 on v3

--- a/solution.py
+++ b/solution.py
@@ -40,23 +40,21 @@
     lax.fori_loop(0, (high - low) // step, run, 0)
 
 
-def along_y(tiles, weights, shift, edges):
+def beside(tiles, shift, edges=True):
     mains, halo = tiles[:3], tiles[3]
     lane = lanes()
-    out = []
+    below, above = [], []
     for c in range(3):
         near = pltpu.roll(halo, 112 - 32 * c, 1)
-        below = pltpu.roll(jnp.where(lane >= 128 - shift, near, mains[c]), shift, 1)
-        above = pltpu.roll(jnp.where(lane < shift, near, mains[c]), 128 - shift, 1)
-        out.append(mains[c] + weights[c] * (below + above))
+        below.append(pltpu.roll(jnp.where(lane >= 128 - shift, near, mains[c]), shift, 1))
+        above.append(pltpu.roll(jnp.where(lane < shift, near, mains[c]), 128 - shift, 1))
     if edges:
         near, place = pack(mains), lane % 32
-        below = pltpu.roll(jnp.where((place >= 16 - shift) & (place < 16), near, halo), shift, 1)
-        above = pltpu.roll(
-            jnp.where((place >= 16) & (place < 16 + shift), near, halo), 128 - shift, 1
-        )
-        out.append(halo + weights[3] * (below + above))
-    return out
+        low = (place >= 16 - shift) & (place < 16)
+        high = (place >= 16) & (place < 16 + shift)
+        below.append(pltpu.roll(jnp.where(low, near, halo), shift, 1))
+        above.append(pltpu.roll(jnp.where(high, near, halo), 128 - shift, 1))
+    return below, above
 
 
 def factors(base, doubled):
@@ -218,15 +216,24 @@
     def row_inside(x, count):
         return jnp.logical_not(((x < 0) & (tx == 0)) | ((x >= count) & (tx == ntx - 1)))
 
+    def keep_beside(ref, pair, r, shift):
+        below, above = beside([pair[0]] * 3 + [pair[1]], shift)
+        for t in range(2):
+            ref[0, t, r], ref[1, t, r], ref[2, t, r] = pair[t], below[3 * t], above[3 * t]
+
     def fine_fields(x):
+        pairs_a, pairs_av = [], []
         for t in range(2):
             tile = cf[t, x + CO]
             keep = inside[t] & row_inside(x, LX)
             active = jnp.where(keep, jnp.broadcast_to(tile[6:7], (8, 128)), 0.0)
-            a[t, x + FO] = active
-            av[t, x + FO] = active * tile
+            pairs_a.append(active)
+            pairs_av.append(active * tile)
+        keep_beside(a, pairs_a, x + FO, 1)
+        keep_beside(av, pairs_av, x + FO, 1)
 
     def coarse_fields(x):
+        pairs_a, pairs_av = [], []
         for t in range(2):
             tile = cf[t, 2 * x + CO] + cf[t, 2 * x + 1 + CO]
             other = jnp.where(lanes() % 2 == 0, pltpu.roll(tile, 127, 1), pltpu.roll(tile, 1, 1))
@@ -234,20 +241,25 @@
             keep = inside[t] & row_inside(x, LX // 2)
             active = jnp.where(keep, 0.25 * jnp.broadcast_to(tile[6:7], (8, 128)), 0.0)
             kv[t, x + KO] = tile
-            ka[t, x + KO] = active
-            kav[t, x + KO] = active * tile
+            pairs_a.append(active)
+            pairs_av.append(active * tile)
+        keep_beside(ka, pairs_a, x + KO, 2)
+        keep_beside(kav, pairs_av, x + KO, 2)
 
     def spread(field, low, high, spacing, shift, offset, flags, products, edges=True):
         weights_y, weights_z = factors(0.25 * spacing, 1), factors(0.5, 2)
 
         def body(x):
             r = x + offset
+            if field is not None:
+                here = [field[c, r] for c in range(4)]
+                below, above = beside(here, shift, edges)
             for k, scale in enumerate((flags, products)):
-                own, beside = scale[0, r], scale[1, r]
-                tiles = [own] * 3 + [beside]
-                if field is not None:
-                    tiles = [tiles[c] * field[c, r] for c in range(4)]
-                for c, tile in enumerate(along_y(tiles, weights_y, shift, edges)):
+                for c in range(4 if edges else 3):
+                    near = [scale[j, c // 3, r] for j in range(3)]
+                    if field is not None:
+                        near = [near[0] * here[c], near[1] * below[c], near[2] * above[c]]
+                    tile = near[0] + weights_y[c] * (near[1] + near[2])
                     g[k, c, r] = along_z(tile, weights_z[c])
 
         rows(low - 1, high + 1, body)
@@ -264,7 +276,7 @@
         def body(x):
             r = x + offset
             for t in range(2):
-                tile, flag, product = visc(t, x), flags[t, r], products[t, r]
+                tile, flag, product = visc(t, x), flags[0, t, r], products[0, t, r]
                 bottom = layers() == 0
                 if t == 1:
                     bottom = bottom & (lanes() < 64)
@@ -292,7 +304,7 @@
         def body(x):
             r = x + FO
             for c in range(4 if edges else 3):
-                flag, visc = a[c // 3, r], cf[c // 3, x + CO]
+                flag, visc = a[0, c // 3, r], cf[c // 3, x + CO]
                 value = field[c, r]
                 left_over = f[c, r] - d[c, r] * value + coupled(c, r, weights_x, flag, visc)
                 finish(c, x, value, left_over)
@@ -322,7 +334,7 @@
                 r = 2 * X + k + FO
                 value = u[c, r]
                 ub[c, r] = value
-                part = coupled(c, r, fine_x, a[0, r], cf[0, 2 * X + k + CO])
+                part = coupled(c, r, fine_x, a[0, 0, r], cf[0, 2 * X + k + CO])
                 part = f[c, r] - d[c, r] * value + part
                 total = part if total is None else total + part
             other = jnp.where(lanes() % 2 == 0, pltpu.roll(total, 127, 1), pltpu.roll(total, 1, 1))
@@ -387,7 +399,7 @@
         def body(x):
             r = x + KO
             for c in range(4):
-                flag, visc = ka[c // 3, r], kv[c // 3, r]
+                flag, visc = ka[0, c // 3, r], kv[c // 3, r]
                 value = kc[c, r]
                 left_over = kr[c, r] - kd[c, r] * value
                 left_over = left_over + coupled(c, r, weights_x, flag, visc)
@@ -442,8 +454,8 @@
         in_specs=[hbm] * 6,
         out_specs=(vmem, vmem),
         scratch_shapes=[
-            fine, fine, tiles(2, CROWS), tiles(2, FROWS), tiles(2, FROWS), fine, fine, fine,
-            tiles(2, 4, FROWS), tiles(2, KROWS), tiles(2, KROWS), tiles(2, KROWS),
+            fine, fine, tiles(2, CROWS), tiles(3, 2, FROWS), tiles(3, 2, FROWS), fine, fine, fine,
+            tiles(2, 4, FROWS), tiles(3, 2, KROWS), tiles(3, 2, KROWS), tiles(2, KROWS),
             coarse, coarse, coarse, coarse,
             tiles(PACK_A), tiles(PACK_A), tiles(PACK_A),
             tiles(PACK_B), tiles(PACK_B), tiles(PACK_B),

time: 49.1 us -> 47.1 us (0.959)
  Pallas kernels: 46.9 us -> 44.9 us
    pallas_call x1, Pallas kernels: 46.9 us -> 44.9 us  [shards(): pl.pallas_call(functools.partial(kernel, ntx, nty), out_shape=(out, out),...]
where the time goes in v4:
time: 47.1 us; the launch traced here: 46.9 us
  Pallas kernels  44.9 us (95%)
  local copies, waits for them, and re-layouts  1.4 us (3%)
  between operations  0.65 us (1%)
    pallas_call x1, Pallas kernels, shards(): pl.pallas_call(functools.partial(kernel, ntx, nty), out_shape=(out, out),...  44.9 us
    unnamed x2, local copies, waits for them, and re-layouts  1.38 us

profile of v4, /device:TPU:25, one launch (start us, length us, event | category | flops | bytes accessed | tf_op | source)
XLA Modules:
  0.0 46.9 jit_solution(3093837106085115889)
XLA Ops:
  0.6 44.9 %shard_map.77 = (f32[3,16,8,128]{3,2,1,0:T(8,128)S(1)}, f32[3,16,8,128]{3,2,1,0:T(8,128)S(1)}) custom-call(f32[16]{0:T(128)} %table.1, f32[3,6,16,128]{3,2,1,0:T(8,128)} %forcing.1, f32[3,6,16,128]{3,2,1,0:T(8,128)} %start.1, s32[16,128]{1,0:T(8,128)} %mask.1, s32[6,16,128]{2,1,0:T(8,128)} %classes.1, f32[16,128]{1,0:T(8,128)} %friction.1), custom_call_target="tpu_custom_call" | custom-call | tf_op jit(solution)/shard_map/pallas_call | solution.py:451
  45.5 0.7 %copy.9 = f32[3,6,16,128]{3,2,1,0:T(8,128)} copy(f32[3,6,16,128]{3,1,2,0:T(8,128)S(1)} %get-tuple-element.8) | data formatting | bytes 294912
  46.2 0.7 %copy.8 = f32[3,6,16,128]{3,2,1,0:T(8,128)} copy(f32[3,6,16,128]{3,1,2,0:T(8,128)S(1)} %get-tuple-element.9) | data formatting | bytes 294912
  (1 shorter events, 0.0 us)
